TPU v7x, 128 devices: a whole 4x4x4 slice. The times are simulated.
128 devices in a mesh: seq: 32 (over x, z, core), head: 4 (over y).
Axes of the slice: x: 4, y: 4, z: 4, core: 2. Of those that a mesh axis runs over, the one named last changes fastest.
Arguments:
- layer_input: bfloat16 [16384, 4096], P('seq', 'head'), may hold values from -6 to 6
- query_rows: bfloat16 [16384, 4096], P('seq', 'head'), may hold values from -6 to 6
- key_rows: bfloat16 [16384, 4096], P('seq', 'head'), may hold values from -6 to 6
- value_rows: bfloat16 [16384, 4096], P('seq', 'head'), may hold values from -28 to 28
- out_weight: bfloat16 [4096, 4096], P('head'), may hold values from -0.09375 to 0.09375
- norm_gain: float32 [4096], P('head'), may hold values from 0.1 to 1.9
- cotangent: bfloat16 [16384, 4096], P('seq', 'head'), may hold values from -0.09375 to 0.09375
Outputs:
- projection_gradient: float32 [4096, 3, 4096], P('seq', None, 'head')
- output_gradient: float32 [4096, 4096], P('head', 'seq')
All inputs are finite; a program needn't handle non-finite values.
Results may differ from a plain program's by a relative error of at most 0.023.
Values may be sent and summed in bfloat16 or wider, within the bound.
A program may use at most 192 MiB of HBM per device.

v0:
```python
import jax
import jax.numpy as jnp
from jax import lax
from jax.sharding import PartitionSpec as P

HEAD_DIM = 128


def entering(array, axis, combine, identity, reverse):
    size, position = (lax.axis_size(axis), lax.axis_index(axis))
    everything = lax.all_gather(array.astype(jnp.bfloat16), axis)
    start = jnp.broadcast_to(jnp.asarray(identity, array.dtype), array.shape)

    def lap(k, before):
        at = size - 1 - k if reverse else k
        reached = at > position if reverse else at < position
        new = combine(before, everything[at].astype(array.dtype))
        return jnp.where(reached, new, before)

    return lax.fori_loop(0, size, lap, start)


def lower_mask(count):
    rows = lax.broadcasted_iota(jnp.int32, (count, count), 0)
    cols = lax.broadcasted_iota(jnp.int32, (count, count), 1)
    return rows >= cols


def body(layer_input, query_rows, key_rows, value_rows, out_weight, norm_gain, cotangent):
    gathered_input, gathered_cot = (
        lax.all_gather(layer_input, "head", axis=1, tiled=True),
        lax.all_gather(cotangent, "head", axis=1, tiled=True),
    )
    tokens = query_rows.shape[0]
    width = query_rows.shape[1]
    heads = width // HEAD_DIM
    queries = query_rows.reshape(tokens, heads, HEAD_DIM)
    key_heads = key_rows.reshape(tokens, heads, HEAD_DIM)
    value_heads = value_rows.reshape(tokens, heads, HEAD_DIM)
    gain = norm_gain.reshape(heads, HEAD_DIM)
    lower = lower_mask(tokens)[None]
    block_state = jnp.einsum(
        "thd,the->hde", key_heads, value_heads, preferred_element_type=jnp.float32
    )
    state_in = entering(block_state, "seq", jnp.add, jnp.zeros_like(block_state), False)
    state_low = state_in.astype(jnp.bfloat16)
    scores = jnp.einsum("thd,shd->hts", queries, key_heads, preferred_element_type=jnp.float32)
    scores = jnp.where(lower, scores, 0.0).astype(jnp.bfloat16)
    attention = jnp.einsum("hts,she->the", scores, value_heads, preferred_element_type=jnp.float32)
    attention = attention + jnp.einsum(
        "thd,hde->the", queries, state_low, preferred_element_type=jnp.float32
    )
    rms_value = jnp.sqrt(jnp.mean(attention * attention, axis=-1, keepdims=True) + 1e-05)
    normed = attention / rms_value
    gated = (normed * gain).astype(jnp.bfloat16).reshape(tokens, width)
    gated_grad = jnp.einsum(
        "tj,cj->tc", gathered_cot, out_weight, preferred_element_type=jnp.float32
    )
    scaled = gated_grad.reshape(tokens, heads, HEAD_DIM) * gain
    inner = jnp.mean(scaled * normed, axis=-1, keepdims=True)
    pre_grad = ((scaled - normed * inner) / rms_value).astype(jnp.bfloat16)
    mixing = jnp.einsum("the,she->hts", pre_grad, value_heads, preferred_element_type=jnp.float32)
    mixing = jnp.where(lower, mixing, 0.0).astype(jnp.bfloat16)
    query_grad = jnp.einsum("hts,shd->thd", mixing, key_heads, preferred_element_type=jnp.float32)
    query_grad = query_grad + jnp.einsum(
        "the,hde->thd", pre_grad, state_low, preferred_element_type=jnp.float32
    )
    query_grad = query_grad.astype(jnp.bfloat16).reshape(tokens, width)
    grad_block = jnp.einsum("thd,the->hde", queries, pre_grad, preferred_element_type=jnp.float32)
    owned_rows = gathered_input.shape[1] // lax.axis_size("seq")
    grad_state = entering(grad_block, "seq", jnp.add, jnp.zeros_like(grad_block), True)
    grad_low = grad_state.astype(jnp.bfloat16)
    key_grad = jnp.einsum("hts,thd->shd", mixing, queries, preferred_element_type=jnp.float32)
    key_grad = key_grad + jnp.einsum(
        "she,hde->shd", value_heads, grad_low, preferred_element_type=jnp.float32
    )
    value_grad = jnp.einsum("hts,the->she", scores, pre_grad, preferred_element_type=jnp.float32)
    value_grad = value_grad + jnp.einsum(
        "shd,hde->she", key_heads, grad_low, preferred_element_type=jnp.float32
    )
    key_grad, value_grad = (
        key_grad.astype(jnp.bfloat16).reshape(tokens, width),
        value_grad.astype(jnp.bfloat16).reshape(tokens, width),
    )
    stacked = jnp.concatenate([query_grad, key_grad, value_grad], axis=1)
    term = jnp.einsum("tc,tj->cj", gathered_input, stacked, preferred_element_type=jnp.float32)
    projection_gradient = lax.psum_scatter(
        term.reshape(lax.axis_size("seq") * owned_rows, -1, width).astype(jnp.bfloat16),
        "seq",
        scatter_dimension=0,
        tiled=True,
    ).astype(jnp.float32)
    out_term = jnp.einsum("tc,tj->cj", gated, gathered_cot, preferred_element_type=jnp.float32)
    output_gradient = lax.psum_scatter(
        out_term.astype(jnp.bfloat16), "seq", scatter_dimension=1, tiled=True
    ).astype(jnp.float32)
    return (projection_gradient, output_gradient)


def solution(mesh):
    placed = (
        P("seq", "head"),
        P("seq", "head"),
        P("seq", "head"),
        P("seq", "head"),
        P("head", None),
        P("head"),
        P("seq", "head"),
    )
    return jax.shard_map(
        body,
        mesh=mesh,
        in_specs=placed,
        out_specs=(P("seq", None, "head"), P("head", "seq")),
        check_vma=False,
    )
```

profile of v0, /device:TPU:0, one launch (start us, length us, event | category | flops | bytes accessed | tf_op | source)
XLA Modules:
  0.0 486.1 jit_solution(13752435765613586975)
XLA Ops:
  7.2 2.6 copy.57
  9.8 2.4 copy.32
  12.3 2.4 convolution_convert_fusion.3
  15.6 2.5 select_convert_fusion.1
  18.2 2.0 copy-done.3
  20.2 2.9 fusion.8
  23.1 47.3 %all-gather.11.cloned.1.call-done = bf16[256,128,128]{2,1,0:T(8,128)(2,1)} async-done(((bf16[8,128,128]{2,1,0:T(8,128)(2,1)}), bf16[256,128,128]{2,1,0:T(8,128)(2,1)}) %all-gather.11.cloned.1.call-update) | async-done | bytes 8388624 | tf_op jit(solution)/shard_map/all_gather | solution.py:11
  70.3 40.3 %while.30 = (s32[]{:T(128)}, f32[8,128,128]{2,1,0:T(8,128)S(1)}, s32[]{:T(128)}, bf16[32,8,128,128]{3,2,1,0:T(8,128)(2,1)}, s32[]{:T(128)}, /*index=5*/s32[]{:T(128)}) while((s32[]{:T(128)}, f32[8,128,128]{2,1,0:T(8,128)S(1)}, s32[]{:T(128)}, bf16[32,8,128,128]{3,2,1,0:T(8,128)(2,1)}, s32[]{:T(128)}, /*index=5*/s32[]{:T(128)}) %tuple.94), condition=%wide.region_1.2_spmd.clone, body=%wide.region_0.1_spmd.clone.sunk | while | flops 524292 | bytes 1310821 | solution.py:20
  79.1 1.3 add_select_fusion.4
  80.4 1.3 add_select_fusion.4
  83.0 1.3 add_select_fusion.4
  110.7 3.5 multiply_reduce_fusion.1
  114.3 5.5 %all-gather.7.cloned.1.call-done = bf16[512,4096]{1,0:T(8,128)(2,1)} async-done(((bf16[512,1024]{1,0:T(8,128)(2,1)}), bf16[512,4096]{1,0:T(8,128)(2,1)}) %all-gather.7.cloned.1.call-update) | async-done | bytes 4194320 | tf_op jit(solution)/shard_map/all_gather | solution.py:32
  119.8 9.9 %multiply_reduce_fusion = (f32[512,8]{0,1:T(8,128)S(1)}, f32[512,1024]{0,1:T(8,128)S(1)}) fusion(f32[8,128]{1,0:T(8,128)S(1)} %bitcast.131, f32[512,8,128]{0,2,1:T(8,128)} %get-tuple-element.246, f32[512,8]{0,1:T(8,128)S(1)} %add_sqrt_fusion, bf16[512,4096]{1,0:T(8,128)(2,1)} %all-gather.7.cloned.1.call-done, bf16[1024,4096]{1,0:T(8,128)(2,1)} %param.15), kind=kOutput, calls=%fused_computation.19 | convolution fusion | flops 4297060352 | bytes 16814080 | tf_op jit(solution)/shard_map/reshape | solution.py:59
  129.7 1.6 multiply_convert_fusion
  133.5 10.2 %convolution_convert_fusion.1 = bf16[1024,4096]{1,0:T(8,128)(2,1)} fusion(bf16[512,1024]{0,1:T(8,128)(2,1)} %bitcast.125, bf16[512,4096]{1,0:T(8,128)(2,1)} %all-gather.7.cloned.1.call-done), kind=kOutput, calls=%fused_computation.5 | convolution fusion | flops 4299161600 | bytes 13631488 | tf_op jit(solution)/shard_map/tc,tj->cj/dot_general | solution.py:93
  143.8 12.0 %copy.52 = bf16[1024,4096]{0,1:T(8,128)(2,1)} copy(bf16[1024,4096]{1,0:T(8,128)(2,1)} %convolution_convert_fusion.1) | data formatting | bytes 16777216
  155.8 4.6 select_convert_fusion
  160.4 4.0 fusion.35
  164.4 1.4 fusion.6
  167.0 2.0 fusion.36
  169.0 17.2 %all-gather.13.cloned.1.call-done = bf16[256,128,128]{2,1,0:T(8,128)(2,1)} async-done(((bf16[8,128,128]{2,1,0:T(8,128)(2,1)}), bf16[256,128,128]{2,1,0:T(8,128)(2,1)}) %all-gather.13.cloned.1.call-update) | async-done | bytes 8388624 | tf_op jit(solution)/shard_map/all_gather | solution.py:11
  186.2 40.5 %while.31 = (s32[]{:T(128)}, f32[8,128,128]{2,1,0:T(8,128)S(1)}, s32[]{:T(128)}, bf16[32,8,128,128]{3,2,1,0:T(8,128)(2,1)}, s32[]{:T(128)}, /*index=5*/s32[]{:T(128)}, s32[]{:T(128)}, s32[]{:T(128)}) while((s32[]{:T(128)}, f32[8,128,128]{2,1,0:T(8,128)S(1)}, s32[]{:T(128)}, bf16[32,8,128,128]{3,2,1,0:T(8,128)(2,1)}, s32[]{:T(128)}, ...), condition=%wide.region_5.6_spmd.clone, body=%wide.region_4.5_spmd.clone.sunk | while | flops 524296 | bytes 1310883 | solution.py:20
  196.4 1.3 add_select_fusion.5
  198.9 1.3 add_select_fusion.5
  229.9 1.8 fusion.5
  231.7 3.8 all-gather.9.cloned.1.call-done
  235.5 21.9 %convolution_convert_fusion = bf16[3072,4096]{1,0:T(8,128)(2,1)} fusion(bf16[512,4096]{1,0:T(8,128)(2,1)} %all-gather.9.cloned.1.call-done, bf16[512,1024]{0,1:T(8,128)(2,1)S(1)} %bitcast.126, bf16[512,1024]{0,1:T(8,128)(2,1)} %bitcast.127, bf16[512,1024]{0,1:T(8,128)(2,1)S(1)} %bitcast.124), kind=kOutput, calls=%fused_computation.2 | convolution fusion | flops 12906921984 | bytes 32505856 | tf_op jit(solution)/shard_map/tc,tj->cj/dot_general | solution.py:86
  257.5 33.1 %copy.46 = bf16[4096,3,1024]{2,0,1:T(8,128)(2,1)} copy(bf16[4096,3,1024]{0,2,1:T(8,128)(2,1)} %bitcast.121) | data formatting | bytes 50331648 | tf_op jit(solution)/shard_map/convert_element_type | solution.py:88
  290.6 41.7 %reduce-scatter.7.cloned.1.call-done = bf16[128,1024]{1,0:T(8,128)(2,1)} async-done(((bf16[4096,1024]{1,0:T(8,128)(2,1)}), bf16[128,1024]{1,0:T(8,128)(2,1)}) %reduce-scatter.7.cloned.1.call-update) | async-done | bytes 262160
  334.2 142.5 %reduce-scatter.5.cloned.1.call-done = bf16[128,3,1024]{2,0,1:T(8,128)(2,1)} async-done(((bf16[4096,3,1024]{2,0,1:T(8,128)(2,1)}), bf16[128,3,1024]{2,0,1:T(8,128)(2,1)}) %reduce-scatter.5.cloned.1.call-update) | async-done | bytes 786448 | tf_op jit(solution)/shard_map/reduce_scatter | solution.py:87
  476.8 2.5 convert_element_type.95
  (105 shorter events, 82.3 us)
Async XLA Ops:
  7.2 8.4 %copy-start = (bf16[512,1024]{1,0:T(8,128)(2,1)S(1)}, bf16[512,1024]{1,0:T(8,128)(2,1)}, u32[]{:S(2)}) copy-start(bf16[512,1024]{1,0:T(8,128)(2,1)} %param.12) | copy-start | bytes 3145732
  7.2 5.1 %copy-start.7 = (bf16[512,1024]{1,0:T(8,128)(2,1)S(1)}, bf16[512,1024]{1,0:T(8,128)(2,1)}, u32[]{:S(2)}) copy-start(bf16[512,1024]{1,0:T(8,128)(2,1)} %param.14) | copy-start | bytes 3145732
  7.2 63.1 %all-gather.11.cloned.1.call-start = ((), (), s32[]{:S(2)}) async-start(), calls=%async_computation.5 | async-start | bytes 8650752 | tf_op jit(solution)/shard_map/all_gather | solution.py:11
  14.7 105.1 %all-gather.7.cloned.1.call-start = ((), (), s32[]{:S(2)}) async-start(), calls=%async_computation.2 | async-start | bytes 5242880 | tf_op jit(solution)/shard_map/all_gather | solution.py:32
  15.5 170.8 %all-gather.13.cloned.1.call-start = ((), (), s32[]{:S(2)}) async-start(), calls=%async_computation.6 | async-start | bytes 8650752 | tf_op jit(solution)/shard_map/all_gather | solution.py:11
  18.2 2.0 copy-start.3
  110.7 9.1 %copy-start.11 = (f32[1024]{0:T(1024)S(1)}, f32[1024]{0:T(1024)}, u32[]{:S(2)}) copy-start(f32[1024]{0:T(1024)} %param.16) | copy-start | bytes 12292
  119.8 10.0 %copy-start.2 = (f32[512,8,128]{0,2,1:T(8,128)S(1)}, f32[512,8,128]{0,2,1:T(8,128)}, u32[]{:S(2)}) copy-start(f32[512,8,128]{0,2,1:T(8,128)} %get-tuple-element.246) | copy-start | bytes 6291460
  132.7 102.8 %all-gather.9.cloned.1.call-start = ((), (), s32[]{:S(2)}) async-start(), calls=%async_computation.3 | async-start | bytes 5242880 | tf_op jit(solution)/shard_map/all_gather | solution.py:31
  133.3 199.0 %reduce-scatter.7.cloned.1.call-start = ((), (), s32[]{:S(2)}) async-start(), calls=%async_computation.7 | async-start | bytes 8650752
  160.4 316.4 %reduce-scatter.5.cloned.1.call-start = ((), (), s32[]{:S(2)}) async-start(), calls=%async_computation.4 | async-start | bytes 25952256 | tf_op jit(solution)/shard_map/reduce_scatter | solution.py:87
  164.4 2.6 copy-start.4
  169.0 57.7 %copy-start.8 = (bf16[512,1024]{1,0:T(8,128)(2,1)S(1)}, bf16[512,1024]{1,0:T(8,128)(2,1)}, u32[]{:S(2)}) copy-start(bf16[512,1024]{1,0:T(8,128)(2,1)} %param.14) | copy-start | bytes 3145732
  226.7 1.6 copy-start.6
  226.8 1.8 copy-start.9
  226.8 3.1 copy-start.5
  229.9 5.6 %copy-start.10 = (bf16[512,8,128]{0,2,1:T(8,128)(2,1)S(1)}, bf16[512,8,128]{0,2,1:T(8,128)(2,1)}, u32[]{:S(2)}) copy-start(bf16[512,8,128]{0,2,1:T(8,128)(2,1)} %fusion.6) | copy-start | bytes 3145732
  290.5 188.7 %copy-start.1 = (bf16[512,1024]{1,0:T(8,128)(2,1)S(1)}, bf16[512,1024]{1,0:T(8,128)(2,1)}, u32[]{:S(2)}) copy-start(bf16[512,1024]{1,0:T(8,128)(2,1)} %param.12) | copy-start | bytes 3145732
Sparse Core Ops, SparseCore 0:
  14.8 55.4 all-gather.10
  72.0 47.7 all-gather.6
  132.8 53.3 all-gather.12
  187.8 47.7 all-gather.8
  239.1 93.1 reduce-scatter.6
  336.6 140.1 reduce-scatter.4
where the time goes:
time: 490 us; the launch traced here: 486 us
  waiting for transfers between devices  259 us (53%)
  other arithmetic  84.3 us (17%)
  matrix products  68.8 us (14%)
  local copies, waits for them, and re-layouts  57.4 us (12%)
  between operations  14.3 us (3%)
    reduce_scatter x1, waiting for transfers between devices, body(): lax.psum_scatter(term.reshape(lax.axis_size('seq') * owned_rows, -1, widt...  143 us
    select_n x64, other arithmetic, lap(): return jnp.where(reached, new, before)  79.3 us
    all_gather x2, waiting for transfers between devices, entering(): everything = lax.all_gather(array.astype(jnp.bfloat16), axis)  64.5 us
    unnamed x7, waiting for transfers between devices  43 us
    convert_element_type x1, local copies, waits for them, and re-layouts, body(): term.reshape(lax.axis_size('seq') * owned_rows, -1, width)  33.1 us
    dot_general x1, matrix products, body(): jnp.einsum('tc,tj->cj', gathered_input, stacked, preferred_element_type=j...  21.9 us
    unnamed x27, local copies, waits for them, and re-layouts  21 us
    dot_general x1, matrix products, body(): jnp.einsum('tc,tj->cj', gated, gathered_cot, preferred_element_type=jnp.f...  10.2 us
  transfers between devices with their start and end apart: 6, of which 6 were waited for; matrix products, arithmetic and copies ran while one was open for 38% of the time, Pallas kernels for 0%

commit v1 on v0

--- a/solution.py
+++ b/solution.py
@@ -1,9 +1,16 @@
 import jax
 import jax.numpy as jnp
 from jax import lax
+from jax.experimental import pallas as pl
+from jax.experimental.pallas import tpu as pltpu
 from jax.sharding import PartitionSpec as P
 
 HEAD_DIM = 128
+F32 = jnp.float32
+BF16 = jnp.bfloat16
+MESH_ID = pl.DeviceIdType.MESH
+COLOURS = ((True, 1), (True, -1), (False, 1), (False, -1))
+RING = 4
 
 
 def entering(array, axis, combine, identity, reverse):
@@ -26,14 +33,185 @@
     return rows >= cols
 
 
+def reduce_kernel(
+    left_hbm, right_hbm, proj_ref, out_ref,
+    lown, lpar, rown, rpar, s1, r1, acc, s2, r2,
+    load_sem, ps_sem, pr_sem, s1_send, s1_recv, s2_send, s2_recv,
+):
+    me = lax.axis_index("seq")
+    core = lax.rem(me, 2)
+    z = lax.rem(lax.div(me, 2), RING)
+    x = lax.div(me, 2 * RING)
+    tokens = lown.shape[-1]
+    cols = s1.shape[-1]
+    rows = RING * HEAD_DIM
+
+    def at(x_, z_, core_):
+        return {"seq": x_ * (2 * RING) + z_ * 2 + core_}
+
+    def step_of(is_z, sign):
+        if is_z:
+            return at(x, lax.rem(z + sign + RING, RING), core)
+        return at(lax.rem(x + sign + RING, RING), z, core)
+
+    partner = at(x, z, 1 - core)
+
+    loads = [pltpu.make_async_copy(left_hbm.at[i], lown.at[i], load_sem.at[i]) for i in range(2)]
+    loads += [
+        pltpu.make_async_copy(right_hbm.at[i], rown.at[i], load_sem.at[2 + i]) for i in range(4)
+    ]
+    for i in (0, 2, 1, 3, 4, 5):
+        loads[i].start()
+
+    barrier = pltpu.get_barrier_semaphore()
+    for who in [partner] + [step_of(is_z, sign) for is_z, sign in COLOURS]:
+        pl.semaphore_signal(barrier, inc=1, device_id=who, device_id_type=MESH_ID)
+    pl.semaphore_wait(barrier, 5)
+
+    swaps = [
+        pltpu.make_async_remote_copy(
+            lown.at[i, :, :, 1 - core], lpar.at[i], ps_sem.at[i], pr_sem.at[i],
+            device_id=partner, device_id_type=MESH_ID)
+        for i in range(2)
+    ] + [
+        pltpu.make_async_remote_copy(
+            rown.at[i], rpar.at[i], ps_sem.at[2 + i], pr_sem.at[2 + i],
+            device_id=partner, device_id_type=MESH_ID)
+        for i in range(4)
+    ]
+    for i in (0, 2, 1, 3, 4, 5):
+        loads[i].wait()
+        swaps[i].start()
+    for i in (0, 2, 1, 3, 4, 5):
+        swaps[i].wait_recv()
+
+    def term(comp, colour, d):
+        side = lax.div(comp + 3, 4)
+        cut = slice(colour * cols, (colour + 1) * cols)
+        if COLOURS[colour][0]:
+            mine, other = lown[side, :, d, core], lpar[side, :, d]
+        else:
+            mine, other = lown[side, d, :, core], lpar[side, d]
+        value = jnp.dot(mine.reshape(rows, tokens), rown[comp, :, cut], preferred_element_type=F32)
+        return value + jnp.dot(
+            other.reshape(rows, tokens), rpar[comp, :, cut], preferred_element_type=F32
+        )
+
+    def first_hop(k, comp, colour):
+        source = s1.at[comp, colour] if k == 0 else r1.at[k - 1, comp, colour]
+        return pltpu.make_async_remote_copy(
+            source, r1.at[k, comp, colour],
+            s1_send.at[k, comp, colour], s1_recv.at[k, comp, colour],
+            device_id=step_of(*COLOURS[colour]), device_id_type=MESH_ID)
+
+    def second_hop(k, comp, colour):
+        is_z, sign = COLOURS[colour]
+        source = s2.at[comp, colour] if k == 0 else r2.at[k - 1, comp, colour]
+        return pltpu.make_async_remote_copy(
+            source, r2.at[k, comp, colour],
+            s2_send.at[k, comp, colour], s2_recv.at[k, comp, colour],
+            device_id=step_of(not is_z, sign), device_id_type=MESH_ID)
+
+    for k in range(RING):
+        @pl.loop(0, 4)
+        def _(comp, k=k):
+            for colour, (is_z, sign) in enumerate(COLOURS):
+                place = z if is_z else x
+                d = lax.rem(place - sign * (1 + k) + 2 * RING, RING)
+                value = term(comp, colour, d)
+                if k:
+                    first_hop(k - 1, comp, colour).wait_recv()
+                    value = value + r1[k - 1, comp, colour].astype(F32)
+                if k == 0:
+                    s1[comp, colour] = value.astype(BF16)
+                elif k < RING - 1:
+                    r1[k - 1, comp, colour] = value.astype(BF16)
+                else:
+                    acc[comp, colour] = value.reshape(RING, HEAD_DIM, cols)
+                    place = x if is_z else z
+                    e = lax.rem(place - sign + 2 * RING, RING)
+                    s2[comp, colour] = acc[comp, colour, e].astype(BF16)
+            for colour in range(4):
+                if k < RING - 1:
+                    first_hop(k, comp, colour).start()
+                else:
+                    second_hop(0, comp, colour).start()
+
+    def second_value(k, comp, colour):
+        is_z, sign = COLOURS[colour]
+        place = x if is_z else z
+        e = lax.rem(place - sign * (1 + k) + 2 * RING, RING)
+        second_hop(k - 1, comp, colour).wait_recv()
+        return acc[comp, colour, e] + r2[k - 1, comp, colour].astype(F32)
+
+    for k in range(1, RING - 1):
+        @pl.loop(0, 4)
+        def _(comp, k=k):
+            for colour in range(4):
+                r2[k - 1, comp, colour] = second_value(k, comp, colour).astype(BF16)
+            for colour in range(4):
+                second_hop(k, comp, colour).start()
+
+    for colour in range(4):
+        cut = slice(colour * cols, (colour + 1) * cols)
+        out_ref[cut, :] = second_value(RING - 1, 0, colour).T
+
+    @pl.loop(1, 4)
+    def _(comp):
+        for colour in range(4):
+            cut = slice(colour * cols, (colour + 1) * cols)
+            proj_ref[comp - 1, :, cut] = second_value(RING - 1, comp, colour)
+
+    for swap in swaps:
+        swap.wait_send()
+
+    @pl.loop(0, 4)
+    def _(comp):
+        for colour in range(4):
+            for k in range(RING - 1):
+                first_hop(k, comp, colour).wait_send()
+                second_hop(k, comp, colour).wait_send()
+
+
+def reduce_terms(left, right):
+    tokens, width = right.shape[1:]
+    cols = width // 4
+    dma = pltpu.SemaphoreType.DMA
+    return pl.pallas_call(
+        reduce_kernel,
+        out_shape=(
+            jax.ShapeDtypeStruct((3, HEAD_DIM, width), F32),
+            jax.ShapeDtypeStruct((width, HEAD_DIM), F32),
+        ),
+        in_specs=[pl.BlockSpec(memory_space=pl.ANY)] * 2,
+        out_specs=(pl.BlockSpec(memory_space=pltpu.VMEM),) * 2,
+        scratch_shapes=[
+            pltpu.VMEM(left.shape, BF16),
+            pltpu.VMEM((2, RING, RING, HEAD_DIM, tokens), BF16),
+            pltpu.VMEM((4, tokens, width), BF16),
+            pltpu.VMEM((4, tokens, width), BF16),
+            pltpu.VMEM((4, 4, RING * HEAD_DIM, cols), BF16),
+            pltpu.VMEM((RING - 1, 4, 4, RING * HEAD_DIM, cols), BF16),
+            pltpu.VMEM((4, 4, RING, HEAD_DIM, cols), F32),
+            pltpu.VMEM((4, 4, HEAD_DIM, cols), BF16),
+            pltpu.VMEM((RING - 1, 4, 4, HEAD_DIM, cols), BF16),
+            dma((6,)), dma((6,)), dma((6,)),
+            dma((RING - 1, 4, 4)), dma((RING - 1, 4, 4)),
+            dma((RING - 1, 4, 4)), dma((RING - 1, 4, 4)),
+        ],
+        compiler_params=pltpu.CompilerParams(
+            collective_id=0, has_side_effects=True, vmem_limit_bytes=67043328
+        ),
+        name="reduce_terms",
+    )(left, right)
+
+
 def body(layer_input, query_rows, key_rows, value_rows, out_weight, norm_gain, cotangent):
-    gathered_input, gathered_cot = (
-        lax.all_gather(layer_input, "head", axis=1, tiled=True),
-        lax.all_gather(cotangent, "head", axis=1, tiled=True),
-    )
     tokens = query_rows.shape[0]
     width = query_rows.shape[1]
     heads = width // HEAD_DIM
+    input_t = lax.all_gather(layer_input.T, "head", axis=0, tiled=True)
+    cot_t = lax.all_gather(cotangent.T, "head", axis=0, tiled=True)
     queries = query_rows.reshape(tokens, heads, HEAD_DIM)
     key_heads = key_rows.reshape(tokens, heads, HEAD_DIM)
     value_heads = value_rows.reshape(tokens, heads, HEAD_DIM)
@@ -53,9 +231,7 @@
     rms_value = jnp.sqrt(jnp.mean(attention * attention, axis=-1, keepdims=True) + 1e-05)
     normed = attention / rms_value
     gated = (normed * gain).astype(jnp.bfloat16).reshape(tokens, width)
-    gated_grad = jnp.einsum(
-        "tj,cj->tc", gathered_cot, out_weight, preferred_element_type=jnp.float32
-    )
+    gated_grad = jnp.einsum("jt,cj->tc", cot_t, out_weight, preferred_element_type=jnp.float32)
     scaled = gated_grad.reshape(tokens, heads, HEAD_DIM) * gain
     inner = jnp.mean(scaled * normed, axis=-1, keepdims=True)
     pre_grad = ((scaled - normed * inner) / rms_value).astype(jnp.bfloat16)
@@ -67,7 +243,6 @@
     )
     query_grad = query_grad.astype(jnp.bfloat16).reshape(tokens, width)
     grad_block = jnp.einsum("thd,the->hde", queries, pre_grad, preferred_element_type=jnp.float32)
-    owned_rows = gathered_input.shape[1] // lax.axis_size("seq")
     grad_state = entering(grad_block, "seq", jnp.add, jnp.zeros_like(grad_block), True)
     grad_low = grad_state.astype(jnp.bfloat16)
     key_grad = jnp.einsum("hts,thd->shd", mixing, queries, preferred_element_type=jnp.float32)
@@ -82,19 +257,10 @@
         key_grad.astype(jnp.bfloat16).reshape(tokens, width),
         value_grad.astype(jnp.bfloat16).reshape(tokens, width),
     )
-    stacked = jnp.concatenate([query_grad, key_grad, value_grad], axis=1)
-    term = jnp.einsum("tc,tj->cj", gathered_input, stacked, preferred_element_type=jnp.float32)
-    projection_gradient = lax.psum_scatter(
-        term.reshape(lax.axis_size("seq") * owned_rows, -1, width).astype(jnp.bfloat16),
-        "seq",
-        scatter_dimension=0,
-        tiled=True,
-    ).astype(jnp.float32)
-    out_term = jnp.einsum("tc,tj->cj", gated, gathered_cot, preferred_element_type=jnp.float32)
-    output_gradient = lax.psum_scatter(
-        out_term.astype(jnp.bfloat16), "seq", scatter_dimension=1, tiled=True
-    ).astype(jnp.float32)
-    return (projection_gradient, output_gradient)
+    left = jnp.stack([cot_t, input_t]).reshape(2, RING, RING, 2, HEAD_DIM, tokens)
+    right = jnp.stack([gated, query_grad, key_grad, value_grad])
+    projection_gradient, output_gradient = reduce_terms(left, right)
+    return (projection_gradient.transpose(1, 0, 2), output_gradient)
 
 
 def solution(mesh):

time: 490 us -> 403 us (0.82)
  waiting for transfers between devices: 259 us -> 114 us
  Pallas kernels: 0 us -> 108 us
  matrix products: 68.8 us -> 38.6 us
  local copies, waits for them, and re-layouts: 57.4 us -> 33.2 us
  other arithmetic: 84.3 us -> 90.8 us
    reduce_scatter x1 -> x0, waiting for transfers between devices: 143 us -> none  [body(): lax.psum_scatter(term.reshape(lax.axis_size('seq') * owned_rows, -1, widt...]
    pallas_call x0 -> x1, Pallas kernels: none -> 108 us  [reduce_terms(): pl.pallas_call(reduce_kernel, out_shape=(jax.ShapeDtypeStruct((3, HEAD_DI...]
    unnamed x7 -> x4, waiting for transfers between devices: 43 us -> 1.41 us
    convert_element_type x1 -> x0, local copies, waits for them, and re-layouts: 33.1 us -> none  [body(): term.reshape(lax.axis_size('seq') * owned_rows, -1, width)]
    all_gather x2, waiting for transfers between devices: 9.29 us -> 37.1 us  [the longest x1 30.5 us: body(): input_t = lax.all_gather(layer_input.T, 'head', axis=0, tiled=True)]
    dot_general x2 -> x1, matrix products: 32.2 us -> 10.3 us  [body(): jnp.einsum('jt,cj->tc', cot_t, out_weight, preferred_element_type=jnp.flo...]
    all_gather x0 -> x2, local copies, waits for them, and re-layouts: none -> 13.2 us  [the longest x1 6.62 us: body(): cot_t = lax.all_gather(cotangent.T, 'head', axis=0, tiled=True)]
    all_gather x2, waiting for transfers between devices: 64.5 us -> 75.8 us  [entering(): everything = lax.all_gather(array.astype(jnp.bfloat16), axis)]
  transfers between devices with their start and end apart: 6 -> 4, of which waited for: 6 -> 4; matrix products, arithmetic and copies ran while one was open for 38% -> 23% of each run, Pallas kernels for 0% -> 0%
where the time goes in v1:
time: 403 us; the launch traced here: 401 us
  waiting for transfers between devices  114 us (28%)
  Pallas kernels  108 us (27%)
  other arithmetic  90.8 us (23%)
  matrix products  38.6 us (10%)
  local copies, waits for them, and re-layouts  33.2 us (8%)
  between operations  14 us (3%)
    pallas_call x1, Pallas kernels, reduce_terms(): pl.pallas_call(reduce_kernel, out_shape=(jax.ShapeDtypeStruct((3, HEAD_DI...  108 us
    select_n x64, other arithmetic, lap(): return jnp.where(reached, new, before)  79.3 us
    all_gather x2, waiting for transfers between devices, entering(): everything = lax.all_gather(array.astype(jnp.bfloat16), axis)  75.8 us
    all_gather x1, waiting for transfers between devices, body(): input_t = lax.all_gather(layer_input.T, 'head', axis=0, tiled=True)  30.5 us
    dot_general x1, matrix products, body(): jnp.einsum('jt,cj->tc', cot_t, out_weight, preferred_element_type=jnp.flo...  10.3 us
    unnamed x33, local copies, waits for them, and re-layouts  10.1 us
  transfers between devices with their start and end apart: 4, of which 4 were waited for; matrix products, arithmetic and copies ran while one was open for 23% of the time, Pallas kernels for 0%

profile of v1, /device:TPU:0, one launch (start us, length us, event | category | flops | bytes accessed | tf_op | source)
XLA Modules:
  0.0 400.6 jit_solution(8792279969556228007)
XLA Ops:
  7.2 2.6 copy.69
  9.8 1.6 copy.38
  14.3 2.9 select_convert_fusion.1
  17.1 1.9 copy-done
  19.1 2.9 fusion.3
  21.9 46.3 %all-gather.11.cloned.1.call-done = bf16[256,128,128]{2,1,0:T(8,128)(2,1)} async-done(((bf16[8,128,128]{2,1,0:T(8,128)(2,1)}), bf16[256,128,128]{2,1,0:T(8,128)(2,1)}) %all-gather.11.cloned.1.call-update) | async-done | bytes 8388624 | tf_op jit(solution)/shard_map/all_gather | solution.py:18
  68.2 40.3 %while.30 = (s32[]{:T(128)}, f32[8,128,128]{2,1,0:T(8,128)S(1)}, s32[]{:T(128)}, bf16[32,8,128,128]{3,2,1,0:T(8,128)(2,1)}, s32[]{:T(128)}, /*index=5*/s32[]{:T(128)}) while((s32[]{:T(128)}, f32[8,128,128]{2,1,0:T(8,128)S(1)}, s32[]{:T(128)}, bf16[32,8,128,128]{3,2,1,0:T(8,128)(2,1)}, s32[]{:T(128)}, /*index=5*/s32[]{:T(128)}) %tuple.92), condition=%wide.region_1.2_spmd.clone, body=%wide.region_0.1_spmd.clone.sunk | while | flops 524292 | bytes 1310821 | solution.py:27
  108.6 2.5 multiply_reduce_fusion.1
  111.1 6.6 %all-gather.7.cloned.1.call-done = bf16[4096,512]{0,1:T(8,128)(2,1)} async-done(((bf16[1024,512]{0,1:T(8,128)(2,1)}), bf16[4096,512]{0,1:T(8,128)(2,1)}) %all-gather.7.cloned.1.call-update) | async-done | bytes 4194320 | tf_op jit(solution)/shard_map/all_gather | solution.py:214
  117.7 10.3 %multiply_convert_fusion = (bf16[512,8,128]{0,2,1:T(8,128)(2,1)}, f32[512,8]{0,1:T(8,128)S(1)}, f32[512,1024]{0,1:T(8,128)S(1)}) fusion(f32[8,128]{1,0:T(8,128)S(1)} %bitcast.130, f32[512,8,128]{0,2,1:T(8,128)S(1)} %get-tuple-element.250, f32[512,8]{0,1:T(8,128)S(1)} %add_sqrt_fusion, bf16[4096,512]{0,1:T(8,128)(2,1)} %all-gather.7.cloned.1.call-done, ...), kind=kOutput, calls=%fused_computation.14 | convolution fusion | flops 4298108928 | bytes 17862656 | tf_op jit(solution)/shard_map/jt,cj->tc/dot_general | solution.py:234
  130.9 6.6 %copy.33 = bf16[4096,512]{1,0:T(8,128)(2,1)} copy(bf16[4096,512]{0,1:T(8,128)(2,1)} %all-gather.7.cloned.1.call-done) | data formatting | bytes 8388608 | tf_op jit(solution)/shard_map/all_gather | solution.py:214
  137.5 30.5 %all-gather.9.cloned.1.call-done = bf16[4096,512]{0,1:T(8,128)(2,1)} async-done(((bf16[1024,512]{0,1:T(8,128)(2,1)}), bf16[4096,512]{0,1:T(8,128)(2,1)}) %all-gather.9.cloned.1.call-update) | async-done | bytes 4194320 | tf_op jit(solution)/shard_map/all_gather | solution.py:213
  168.0 6.6 %copy.34 = bf16[4096,512]{1,0:T(8,128)(2,1)} copy(bf16[4096,512]{0,1:T(8,128)(2,1)} %all-gather.9.cloned.1.call-done) | data formatting | bytes 8388608 | tf_op jit(solution)/shard_map/all_gather | solution.py:213
  174.5 7.6 %pad_maximum_fusion.left_hbm = bf16[2,4,4,2,128,512]{5,4,3,2,1,0:T(8,128)(2,1)} fusion(bf16[1,4,4,2,128,512]{5,4,3,2,1,0:T(8,128)(2,1)} %bitcast.118, bf16[1,4,4,2,128,512]{5,4,3,2,1,0:T(8,128)(2,1)} %bitcast.117), kind=kLoop, calls=%fused_computation.2 | loop fusion | flops 4194304 | bytes 16777216 | tf_op jit(solution)/shard_map/stack | solution.py:260
  182.2 1.4 select_convert_fusion
  183.7 1.5 fusion.29
  185.2 1.5 fusion.1
  186.6 2.3 copy.63
  188.9 1.3 copy.62
  190.3 4.3 %fusion.30 = f32[8,128,512]{2,1,0:T(8,128)} fusion(bf16[512,8,128]{0,2,1:T(8,128)(2,1)S(1)} %copy-done.3, bf16[8,512,512]{2,1,0:T(8,128)(2,1)} %copy-done), kind=kOutput, calls=%fused_computation.50 | convolution fusion | flops 536870912 | bytes 7340032 | tf_op jit(solution)/shard_map/hts,the->she/dot_general | solution.py:252
  194.6 29.5 %all-gather.13.cloned.1.call-done = bf16[256,128,128]{2,1,0:T(8,128)(2,1)} async-done(((bf16[8,128,128]{2,1,0:T(8,128)(2,1)}), bf16[256,128,128]{2,1,0:T(8,128)(2,1)}) %all-gather.13.cloned.1.call-update) | async-done | bytes 8388624 | tf_op jit(solution)/shard_map/all_gather | solution.py:18
  224.1 40.7 %while.31 = (s32[]{:T(128)}, f32[8,128,128]{2,1,0:T(8,128)S(1)}, s32[]{:T(128)}, bf16[32,8,128,128]{3,2,1,0:T(8,128)(2,1)}, s32[]{:T(128)}, /*index=5*/s32[]{:T(128)}, s32[]{:T(128)}, s32[]{:T(128)}) while((s32[]{:T(128)}, f32[8,128,128]{2,1,0:T(8,128)S(1)}, s32[]{:T(128)}, bf16[32,8,128,128]{3,2,1,0:T(8,128)(2,1)}, s32[]{:T(128)}, ...), condition=%wide.region_5.6_spmd.clone, body=%wide.region_4.5_spmd.clone.sunk | while | flops 524296 | bytes 1310883 | solution.py:27
  224.1 1.4 add_select_fusion.5
  264.8 3.2 fusion.5
  268.0 1.5 add_convert_fusion
  269.5 1.5 copy.65
  271.0 5.1 %fusion = bf16[512,8,128]{0,2,1:T(8,128)(2,1)} fusion(f32[8,128,512]{2,1,0:T(8,128)} %fusion.5, bf16[8,512,512]{2,1,0:T(8,128)(2,1)} %copy-done.1, bf16[512,1024]{1,0:T(8,128)(2,1)} %param.12), kind=kOutput, calls=%fused_computation.7 | convolution fusion | flops 537919488 | bytes 8388608 | tf_op jit(solution)/shard_map/hts,thd->shd/dot_general | solution.py:248
  276.1 2.3 copy.64
  278.4 3.2 pad_maximum_fusion.1.right_hbm
  281.7 107.8 %reduce_terms.1 = (f32[3,128,1024]{2,1,0:T(8,128)}, f32[1024,128]{1,0:T(8,128)}) custom-call(bf16[2,4,4,2,128,512]{5,4,3,2,1,0:T(8,128)(2,1)} %pad_maximum_fusion.left_hbm, bf16[4,512,1024]{2,1,0:T(8,128)(2,1)} %pad_maximum_fusion.1.right_hbm), custom_call_target="tpu_custom_call" | custom-call | tf_op jit(solution)/shard_map/reduce_terms/pallas_call | solution.py:180
  389.5 2.7 copy.126
  392.2 1.9 copy.127
  (109 shorter events, 83.6 us)
Async XLA Ops:
  7.2 4.2 %copy-start.5 = (bf16[512,1024]{1,0:T(8,128)(2,1)S(1)}, bf16[512,1024]{1,0:T(8,128)(2,1)}, u32[]{:S(2)}) copy-start(bf16[512,1024]{1,0:T(8,128)(2,1)} %param.14) | copy-start | bytes 3145732
  7.2 61.1 %all-gather.11.cloned.1.call-start = ((), (), s32[]{:S(2)}) async-start(), calls=%async_computation.2 | async-start | bytes 8650752 | tf_op jit(solution)/shard_map/all_gather | solution.py:18
  11.4 5.7 %copy-start.7 = (bf16[512,8,128]{0,2,1:T(8,128)(2,1)}, bf16[512,8,128]{0,2,1:T(8,128)(2,1)S(1)}, u32[]{:S(2)}) copy-start(bf16[512,8,128]{0,2,1:T(8,128)(2,1)S(1)} %copy.38) | copy-start | bytes 3145732
  12.6 105.1 %all-gather.7.cloned.1.call-start = ((), (), s32[]{:S(2)}) async-start(), calls=%async_computation | async-start | bytes 5242880 | tf_op jit(solution)/shard_map/all_gather | solution.py:214
  13.4 154.6 %all-gather.9.cloned.1.call-start = ((), (), s32[]{:S(2)}) async-start(), calls=%async_computation.1 | async-start | bytes 5242880 | tf_op jit(solution)/shard_map/all_gather | solution.py:213
  14.1 210.0 %all-gather.13.cloned.1.call-start = ((), (), s32[]{:S(2)}) async-start(), calls=%async_computation.3 | async-start | bytes 8650752 | tf_op jit(solution)/shard_map/all_gather | solution.py:18
  17.1 1.9 copy-start
  108.6 9.1 %copy-start.14 = (f32[1024]{0:T(1024)S(1)}, f32[1024]{0:T(1024)}, u32[]{:S(2)}) copy-start(f32[1024]{0:T(1024)} %param.16) | copy-start | bytes 12292
  128.0 1.5 copy-start.13
  128.5 1.0 copy-start.2
  174.5 7.6 %copy-start.3 = (bf16[512,8,128]{0,2,1:T(8,128)(2,1)S(1)}, bf16[512,8,128]{0,2,1:T(8,128)(2,1)}, u32[]{:S(2)}) copy-start(bf16[512,8,128]{0,2,1:T(8,128)(2,1)} %copy-done.2) | copy-start | bytes 3145732
  174.5 7.6 %copy-start.6 = (bf16[512,1024]{1,0:T(8,128)(2,1)S(1)}, bf16[512,1024]{1,0:T(8,128)(2,1)}, u32[]{:S(2)}) copy-start(bf16[512,1024]{1,0:T(8,128)(2,1)} %param.14) | copy-start | bytes 3145732
  182.2 1.5 copy-start.8
  183.7 3.0 copy-start.1
  185.2 3.8 copy-start.9
  224.1 43.9 %copy-start.4 = (f32[8,128,512]{2,1,0:T(8,128)S(1)}, f32[8,128,512]{2,1,0:T(8,128)}, u32[]{:S(2)}) copy-start(f32[8,128,512]{2,1,0:T(8,128)} %fusion.30) | copy-start | bytes 6291460
  264.8 3.2 copy-start.10
  271.0 7.4 %copy-start.11 = (bf16[1,512,1024]{2,1,0:T(8,128)(2,1)S(1)}, bf16[1,512,1024]{2,1,0:T(8,128)(2,1)}, u32[]{:S(2)}) copy-start(bf16[1,512,1024]{2,1,0:T(8,128)(2,1)} %copy.63) | copy-start | bytes 3145732
  271.0 7.4 %copy-start.12 = (bf16[1,512,1024]{2,1,0:T(8,128)(2,1)S(1)}, bf16[1,512,1024]{2,1,0:T(8,128)(2,1)}, u32[]{:S(2)}) copy-start(bf16[1,512,1024]{2,1,0:T(8,128)(2,1)} %copy.62) | copy-start | bytes 3145732
Sparse Core Ops, SparseCore 0:
  12.7 55.4 all-gather.10
  69.9 47.7 all-gather.6
  119.4 48.5 all-gather.8
  170.7 53.3 all-gather.12

commit v2 on v0

v2 whole, which is shorter than its diff:
```python
import jax
import jax.numpy as jnp
from jax import lax
from jax.experimental import pallas as pl
from jax.experimental.pallas import tpu as pltpu
from jax.sharding import PartitionSpec as P

HEAD_DIM = 128
F32 = jnp.float32
BF16 = jnp.bfloat16
MESH_ID = pl.DeviceIdType.MESH
COLOURS = ((True, 1), (True, -1), (False, 1), (False, -1))
RING = 4
ROW = 8


def dot_nn(a, b):
    return jnp.dot(a, b, preferred_element_type=F32)


def dot_nt(a, b):
    return lax.dot_general(a, b, (((1,), (1,)), ((), ())), preferred_element_type=F32)


def dot_tn(a, b):
    return jnp.dot(a.T, b, preferred_element_type=F32)


def step_kernel(
    x_hbm, q_hbm, k_hbm, v_hbm, w_hbm, gain_ref, cot_hbm,
    proj_ref, out_ref,
    lown, lpar, rown, rpar, qs, ks, vs, wbuf, att, gg, pre, s1, r1, acc, r2,
    blocks, gathered, totals, results, states,
    load_sem, g_send, g_recv, row_send, row_recv, tot_send, tot_recv, res_send, res_recv,
    lp_send, lp_recv, rp_send, rp_recv, s1_send, s1_recv, s2_send, s2_recv,
):
    me = lax.axis_index("seq")
    y = lax.axis_index("head")
    core = lax.rem(me, 2)
    z = lax.rem(lax.div(me, 2), RING)
    x = lax.div(me, ROW)
    j = lax.rem(me, ROW)
    tokens = qs.shape[0]
    width = qs.shape[1]
    half = tokens // 2
    heads = width // HEAD_DIM
    cols = s1.shape[-1]
    rows = RING * HEAD_DIM

    def at(x_, z_, core_):
        return {"seq": x_ * ROW + z_ * 2 + core_}

    def row_peer(j_):
        return {"seq": x * ROW + j_}

    def turn(a, n=RING):
        return lax.rem(a + 2 * n, n)

    def step_of(is_z, sign):
        return at(x, turn(z + sign), core) if is_z else at(turn(x + sign), z, core)

    partner = at(x, z, 1 - core)

    def remote(source, target, send, recv, who):
        return pltpu.make_async_remote_copy(
            source, target, send, recv, device_id=who, device_id_type=MESH_ID)

    def weight_load(n, chunk):
        start = pl.multiple_of(chunk * width, width)
        return pltpu.make_async_copy(
            w_hbm.at[:, pl.ds(start, width)], wbuf.at[n % 2], load_sem.at[5 + n])

    order = (y, turn(y - 1), turn(y + 1), turn(y + 2))
    load_cot = pltpu.make_async_copy(cot_hbm, rown.at[1], load_sem.at[0])
    load_k = pltpu.make_async_copy(k_hbm, ks, load_sem.at[1])
    load_v = pltpu.make_async_copy(v_hbm, vs, load_sem.at[2])
    load_x = pltpu.make_async_copy(x_hbm, rown.at[2], load_sem.at[3])
    load_q = pltpu.make_async_copy(q_hbm, qs, load_sem.at[4])
    for load in (load_cot, load_k, load_v, load_x, load_q):
        load.start()
    weight_load(0, order[0]).start()
    weight_load(1, order[1]).start()

    barrier = pltpu.get_barrier_semaphore()
    peers = [row_peer(turn(j + o, ROW)) for o in range(1, ROW)]
    peers += [at(turn(x + o), z, core) for o in range(1, RING)]
    peers += [{"head": turn(y + 1)}, {"head": turn(y - 1)}]
    for who in peers:
        pl.semaphore_signal(barrier, inc=1, device_id=who, device_id_type=MESH_ID)

    def transpose_in(side, stage):
        for i in range(heads):
            lown[side, y, i // 2, i % 2] = rown[stage, :, i * HEAD_DIM:(i + 1) * HEAD_DIM].T

    load_cot.wait()
    transpose_in(0, 1)
    pl.semaphore_wait(barrier, len(peers))

    def ring(side, sign, message, receiving=False):
        first = 0 if sign > 0 else 2
        part = first if message != 1 else 2 - first
        source = y if message < 2 else turn(y - sign)
        if receiving:
            source = turn(source - sign)
        place = lown.at[side, source, pl.ds(part, 2)]
        n = 0 if sign > 0 else 1
        return remote(
            place, place, g_send.at[side, n, message], g_recv.at[side, n, message],
            {"head": turn(y + sign)})

    def gather_own(side):
        for message in (0, 1):
            for sign in (1, -1):
                ring(side, sign, message).start()

    def gather_pass(side):
        for sign in (1, -1):
            ring(side, sign, 0, True).wait_recv()
            ring(side, sign, 2).start()

    gather_own(0)

    def row_copy(n, o, receiving=False):
        if receiving:
            place = turn(j - o, ROW)
            return remote(blocks.at[n, place], gathered.at[n, place],
                          row_send.at[n, o - 1], row_recv.at[n, o - 1], row_peer(place))
        to = turn(j + o, ROW)
        return remote(blocks.at[n, to], gathered.at[n, j],
                      row_send.at[n, o - 1], row_recv.at[n, o - 1], row_peer(to))

    def total_copy(n, o, receiving=False):
        place = turn(x - o) if receiving else x
        return remote(totals.at[n, place], totals.at[n, place],
                      tot_send.at[n, o - 1], tot_recv.at[n, o - 1], at(turn(x + o), z, core))

    def result_copy(n, o, receiving=False):
        if receiving:
            place = turn(j - o, ROW)
            return remote(results.at[n, place], states.at[n, place],
                          res_send.at[n, o - 1], res_recv.at[n, o - 1], row_peer(place))
        to = turn(j + o, ROW)
        return remote(results.at[n, to], states.at[n, j],
                      res_send.at[n, o - 1], res_recv.at[n, o - 1], row_peer(to))

    def scan_rows(n):
        gathered[n, j] = blocks[n, j]
        for o in range(1, ROW):
            row_copy(n, o).start()

    def scan_totals(n):
        for o in range(1, ROW):
            row_copy(n, o, True).wait_recv()
        total = gathered[n, 0].astype(F32)
        for i in range(1, ROW):
            total = total + gathered[n, i].astype(F32)
        totals[n, x] = total
        for o in range(1, RING):
            total_copy(n, o).start()

    def scan_results(n):
        for o in range(1, RING):
            total_copy(n, o, True).wait_recv()
        running = jnp.zeros((HEAD_DIM, HEAD_DIM), F32)
        for i in range(RING):
            counts = (i > x) if n else (i < x)
            running = running + jnp.where(counts, totals[n, i], 0.0)
        for i in (reversed(range(ROW)) if n else range(ROW)):
            results[n, i] = running.astype(BF16)
            running = running + gathered[n, i].astype(F32)
        states[n, j] = results[n, j]
        for o in range(1, ROW):
            result_copy(n, o).start()

    def scan_end(n):
        for o in range(1, ROW):
            result_copy(n, o, True).wait_recv()

    def head(ref, h):
        return ref[:, pl.ds(pl.multiple_of(h * HEAD_DIM, HEAD_DIM), HEAD_DIM)]

    def put_head(comp, h, value):
        rown[comp, :, pl.ds(pl.multiple_of(h * HEAD_DIM, HEAD_DIM), HEAD_DIM)] = value.astype(BF16)

    load_k.wait()
    load_v.wait()

    @pl.loop(0, heads)
    def _(h):
        blocks[0, h] = dot_tn(head(ks, h), head(vs, h)).astype(BF16)

    scan_rows(0)
    load_x.wait()
    transpose_in(1, 2)
    load_q.wait()
    scan_totals(0)

    lower_left = (
        lax.broadcasted_iota(jnp.int32, (tokens, half), 0)
        >= lax.broadcasted_iota(jnp.int32, (tokens, half), 1)
    )
    lower_right = lower_left[:half]

    def score_slots(h):
        return lax.div(h, 2), lax.rem(h, 2) * 2

    @pl.loop(0, heads)
    def _(h):
        q, k, v = head(qs, h), head(ks, h), head(vs, h)
        left = jnp.where(lower_left, dot_nt(q, k[:half]), 0.0).astype(BF16)
        right = jnp.where(lower_right, dot_nt(q[half:], k[half:]), 0.0).astype(BF16)
        a, b = score_slots(h)
        s1[a, b] = left
        s1[a, b + 1, :half] = right
        att[h, :half] = dot_nn(left[:half], v[:half])
        att[h, half:] = dot_nn(left[half:], v[:half]) + dot_nn(right, v[half:])

    scan_results(0)

    def grad_chunk(n):
        weight_load(n, order[n]).wait()

        @pl.loop(0, RING)
        def _(t):
            w = wbuf[n % 2, pl.ds(pl.multiple_of(t * 2 * HEAD_DIM, 2 * HEAD_DIM), 2 * HEAD_DIM), :]
            value = dot_nn(w, lown[0, order[n]].reshape(width, tokens)).T
            for i in range(2):
                piece = value[:, i * HEAD_DIM:(i + 1) * HEAD_DIM]
                if n:
                    piece = piece + gg[2 * t + i]
                gg[2 * t + i] = piece

        if n + 2 < RING:
            weight_load(n + 2, order[n + 2]).start()

    grad_chunk(0)
    gather_pass(0)
    gather_own(1)

    def normalised(h):
        a = att[h]
        inverse = lax.rsqrt(jnp.mean(a * a, axis=-1, keepdims=True) + 1e-05)
        return a * inverse, inverse

    scan_end(0)

    @pl.loop(0, heads)
    def _(h):
        att[h] = att[h] + dot_nn(head(qs, h), states[0, h])
        normed, _ = normalised(h)
        put_head(0, h, normed * gain_ref[pl.ds(h, 1), :])

    def left_swap(side, piece):
        return remote(lown.at[side, piece, :, 1 - core], lpar.at[side, piece],
                      lp_send.at[side, piece], lp_recv.at[side, piece], partner)

    def right_swap(comp):
        return remote(rown.at[comp], rpar.at[comp], rp_send.at[comp], rp_recv.at[comp], partner)

    right_swap(0).start()
    ring(0, 1, 1, True).wait_recv()
    left_swap(0, order[0]).start()
    left_swap(0, order[1]).start()
    grad_chunk(1)
    ring(0, -1, 1, True).wait_recv()
    left_swap(0, order[2]).start()
    grad_chunk(2)
    ring(0, 1, 2, True).wait_recv()
    ring(0, -1, 2, True).wait_recv()
    left_swap(0, order[3]).start()
    grad_chunk(3)

    @pl.loop(0, heads)
    def _(h):
        normed, inverse = normalised(h)
        u = gg[h] * gain_ref[pl.ds(h, 1), :]
        m = jnp.mean(u * normed, axis=-1, keepdims=True)
        p = ((u - normed * m) * inverse).astype(BF16)
        pre[h] = p
        blocks[1, h] = dot_tn(head(qs, h), p).astype(BF16)

    scan_rows(1)

    def term(comp, colour, d):
        side = lax.div(comp + 3, 4)
        cut = slice(colour * cols, (colour + 1) * cols)
        if COLOURS[colour][0]:
            mine, other = lown[side, :, d, core], lpar[side, :, d]
        else:
            mine, other = lown[side, d, :, core], lpar[side, d]
        value = dot_nn(mine.reshape(rows, tokens), rown[comp, :, cut])
        return value + dot_nn(other.reshape(rows, tokens), rpar[comp, :, cut])

    def first_hop(k, comp, colour):
        source = s1.at[comp, colour] if k == 0 else r1.at[k - 1, comp, colour]
        return remote(source, r1.at[k, comp, colour], s1_send.at[k, comp, colour],
                      s1_recv.at[k, comp, colour], step_of(*COLOURS[colour]))

    def second_hop(k, comp, colour):
        is_z, sign = COLOURS[colour]
        place = x if is_z else z
        source = acc.at[comp, colour, turn(place - sign)] if k == 0 else r2.at[k - 1, comp, colour]
        return remote(source, r2.at[k, comp, colour], s2_send.at[k, comp, colour],
                      s2_recv.at[k, comp, colour], step_of(not is_z, sign))

    def first_step(k, comp):
        for colour, (is_z, sign) in enumerate(COLOURS):
            value = term(comp, colour, turn((z if is_z else x) - sign * (1 + k)))
            if k:
                first_hop(k - 1, comp, colour).wait_recv()
                value = value + r1[k - 1, comp, colour].astype(F32)
            value = value.astype(BF16)
            if k == 0:
                s1[comp, colour] = value
            elif k < RING - 1:
                r1[k - 1, comp, colour] = value
            else:
                acc[comp, colour] = value.reshape(RING, HEAD_DIM, cols)
        for colour in range(4):
            if k < RING - 1:
                first_hop(k, comp, colour).start()
            else:
                second_hop(0, comp, colour).start()

    def second_value(k, comp, colour):
        is_z, sign = COLOURS[colour]
        e = turn((x if is_z else z) - sign * (1 + k))
        second_hop(k - 1, comp, colour).wait_recv()
        return acc[comp, colour, e].astype(F32) + r2[k - 1, comp, colour].astype(F32)

    def second_step(k, comp):
        for colour in range(4):
            r2[k - 1, comp, colour] = second_value(k, comp, colour).astype(BF16)
        for colour in range(4):
            second_hop(k, comp, colour).start()

    scan_totals(1)

    @pl.loop(0, heads)
    def _(h):
        q, k, v, p = head(qs, h), head(ks, h), head(vs, h), pre[h]
        state = states[0, h]
        left = jnp.where(lower_left, dot_nt(p, v[:half]), 0.0).astype(BF16)
        right = jnp.where(lower_right, dot_nt(p[half:], v[half:]), 0.0).astype(BF16)
        old = dot_nt(p, state)
        low = dot_nn(left, k[:half]) + old
        cut = pl.ds(pl.multiple_of(h * HEAD_DIM, HEAD_DIM), HEAD_DIM)
        rown[1, :half, cut] = low[:half].astype(BF16)
        rown[1, half:, cut] = (low[half:] + dot_nn(right, k[half:])).astype(BF16)
        att[h, :half] = dot_tn(left, q)
        att[h, half:] = dot_tn(right, q[half:])
        a, b = score_slots(h)
        gg[h, :half] = dot_tn(s1[a, b], p)
        gg[h, half:] = dot_tn(s1[a, b + 1, :half], p[half:])

    scan_results(1)
    right_swap(1).start()
    for piece in order:
        left_swap(0, piece).wait_recv()
    right_swap(0).wait_recv()
    first_step(0, 0)
    gather_pass(1)
    scan_end(1)

    @pl.loop(0, heads)
    def _(h):
        k, v = head(ks, h), head(vs, h)
        put_head(2, h, att[h] + dot_nt(v, states[1, h]))
        put_head(3, h, gg[h] + dot_nn(k, states[1, h]))

    right_swap(2).start()
    right_swap(3).start()
    first_step(1, 0)
    left_swap(1, order[0]).start()
    ring(1, 1, 1, True).wait_recv()
    left_swap(1, order[1]).start()
    ring(1, -1, 1, True).wait_recv()
    left_swap(1, order[2]).start()
    first_step(2, 0)
    ring(1, 1, 2, True).wait_recv()
    ring(1, -1, 2, True).wait_recv()
    left_swap(1, order[3]).start()
    first_step(3, 0)
    for comp in range(1, 4):
        right_swap(comp).wait_recv()
    for piece in order:
        left_swap(1, piece).wait_recv()

    for k in range(RING):
        @pl.loop(1, 4)
        def _(comp, k=k):
            first_step(k, comp)

        if 0 < k < RING - 1:
            second_step(k, 0)

    for colour in range(4):
        cut = slice(colour * cols, (colour + 1) * cols)
        out_ref[cut, :] = second_value(RING - 1, 0, colour).T

    for k in range(1, RING - 1):
        @pl.loop(1, 4)
        def _(comp, k=k):
            second_step(k, comp)

    @pl.loop(1, 4)
    def _(comp):
        for colour in range(4):
            cut = slice(colour * cols, (colour + 1) * cols)
            proj_ref[comp - 1, :, cut] = second_value(RING - 1, comp, colour)

    for side in range(2):
        for sign in (1, -1):
            for message in range(3):
                ring(side, sign, message).wait_send()
        for piece in order:
            left_swap(side, piece).wait_send()
        for o in range(1, ROW):
            row_copy(side, o).wait_send()
            result_copy(side, o).wait_send()
        for o in range(1, RING):
            total_copy(side, o).wait_send()

    @pl.loop(0, 4)
    def _(comp):
        right_swap(comp).wait_send()
        for colour in range(4):
            for k in range(RING - 1):
                first_hop(k, comp, colour).wait_send()
                second_hop(k, comp, colour).wait_send()


def body(layer_input, query_rows, key_rows, value_rows, out_weight, norm_gain, cotangent):
    tokens, width = query_rows.shape
    heads = width // HEAD_DIM
    cols = width // 4
    dma = pltpu.SemaphoreType.DMA
    square = (HEAD_DIM, HEAD_DIM)
    anywhere = pl.BlockSpec(memory_space=pl.ANY)
    inside = pl.BlockSpec(memory_space=pltpu.VMEM)
    projection_gradient, output_gradient = pl.pallas_call(
        step_kernel,
        out_shape=(
            jax.ShapeDtypeStruct((3, HEAD_DIM, width), F32),
            jax.ShapeDtypeStruct((width, HEAD_DIM), F32),
        ),
        in_specs=[anywhere] * 5 + [inside, anywhere],
        out_specs=(inside, inside),
        scratch_shapes=[
            pltpu.VMEM((2, RING, RING, 2, HEAD_DIM, tokens), BF16),
            pltpu.VMEM((2, RING, RING, HEAD_DIM, tokens), BF16),
            pltpu.VMEM((4, tokens, width), BF16),
            pltpu.VMEM((4, tokens, width), BF16),
            pltpu.VMEM((tokens, width), BF16),
            pltpu.VMEM((tokens, width), BF16),
            pltpu.VMEM((tokens, width), BF16),
            pltpu.VMEM((2, width, width), BF16),
            pltpu.VMEM((heads, tokens, HEAD_DIM), F32),
            pltpu.VMEM((heads, tokens, HEAD_DIM), F32),
            pltpu.VMEM((heads, tokens, HEAD_DIM), BF16),
            pltpu.VMEM((4, 4, RING * HEAD_DIM, cols), BF16),
            pltpu.VMEM((RING - 1, 4, 4, RING * HEAD_DIM, cols), BF16),
            pltpu.VMEM((4, 4, RING, HEAD_DIM, cols), BF16),
            pltpu.VMEM((RING - 1, 4, 4, HEAD_DIM, cols), BF16),
            pltpu.VMEM((2, ROW) + square, BF16),
            pltpu.VMEM((2, ROW) + square, BF16),
            pltpu.VMEM((2, RING) + square, F32),
            pltpu.VMEM((2, ROW) + square, BF16),
            pltpu.VMEM((2, ROW) + square, BF16),
            dma((9,)),
            dma((2, 2, 3)), dma((2, 2, 3)),
            dma((2, ROW - 1)), dma((2, ROW - 1)),
            dma((2, RING - 1)), dma((2, RING - 1)),
            dma((2, ROW - 1)), dma((2, ROW - 1)),
            dma((2, RING)), dma((2, RING)),
            dma((4,)), dma((4,)),
            dma((RING - 1, 4, 4)), dma((RING - 1, 4, 4)),
            dma((RING - 1, 4, 4)), dma((RING - 1, 4, 4)),
        ],
        compiler_params=pltpu.CompilerParams(
            collective_id=0, has_side_effects=True, vmem_limit_bytes=67043328
        ),
        name="linear_attention_backward",
    )(
        layer_input, query_rows, key_rows, value_rows, out_weight,
        norm_gain.reshape(heads, HEAD_DIM), cotangent,
    )
    return (projection_gradient.transpose(1, 0, 2), output_gradient)


def solution(mesh):
    placed = (
        P("seq", "head"),
        P("seq", "head"),
        P("seq", "head"),
        P("seq", "head"),
        P("head", None),
        P("head"),
        P("seq", "head"),
    )
    return jax.shard_map(
        body,
        mesh=mesh,
        in_specs=placed,
        out_specs=(P("seq", None, "head"), P("head", "seq")),
        check_vma=False,
    )
```

time: 490 us -> 172 us (0.35)
  waiting for transfers between devices: 259 us -> 0 us
  Pallas kernels: 0 us -> 168 us
  other arithmetic: 84.3 us -> 0 us
  matrix products: 68.8 us -> 0 us
  local copies, waits for them, and re-layouts: 57.4 us -> 3.58 us
  between operations: 14.3 us -> 0.65 us
    pallas_call x0 -> x1, Pallas kernels: none -> 168 us  [body(): pl.pallas_call(step_kernel, out_shape=(jax.ShapeDtypeStruct((3, HEAD_DIM,...]
    reduce_scatter x1 -> x0, waiting for transfers between devices: 143 us -> none  [body(): lax.psum_scatter(term.reshape(lax.axis_size('seq') * owned_rows, -1, widt...]
    select_n x64 -> x0, other arithmetic: 79.3 us -> none  [lap(): return jnp.where(reached, new, before)]
    all_gather x4 -> x0, waiting for transfers between devices: 73.8 us -> none  [the longest x2 64.5 us: entering(): everything = lax.all_gather(array.astype(jnp.bfloat16), axis)]
    dot_general x14 -> x0, matrix products: 58.8 us -> none  [the longest x1 21.9 us: body(): jnp.einsum('tc,tj->cj', gathered_input, stacked, preferred_element_type=j...]
    unnamed x7 -> x0, waiting for transfers between devices: 43 us -> none
    convert_element_type x2 -> x0, local copies, waits for them, and re-layouts: 33.9 us -> none  [the longest x1 33.1 us: body(): term.reshape(lax.axis_size('seq') * owned_rows, -1, width)]
    unnamed x27 -> x4, local copies, waits for them, and re-layouts: 21 us -> 3.58 us
  transfers between devices with their start and end apart: 6 -> 0, of which waited for: 6 -> 0; matrix products, arithmetic and copies ran while one was open for 38% -> 0% of each run, Pallas kernels for 0% -> 0%
where the time goes in v2:
time: 172 us
  Pallas kernels  168 us (98%)
  local copies, waits for them, and re-layouts  3.58 us (2%)
    pallas_call x1, Pallas kernels, body(): pl.pallas_call(step_kernel, out_shape=(jax.ShapeDtypeStruct((3, HEAD_DIM,...  168 us
    unnamed x4, local copies, waits for them, and re-layouts  3.58 us

profile of v2, /device:TPU:0, one launch (start us, length us, event | category | flops | bytes accessed | tf_op | source)
XLA Modules:
  0.0 172.1 jit_solution(2263667784579905948)
XLA Ops:
  0.6 167.8 %linear_attention_backward.1 = (f32[3,128,1024]{2,1,0:T(8,128)}, f32[1024,128]{1,0:T(8,128)}) custom-call(bf16[512,1024]{1,0:T(8,128)(2,1)} %x_hbm.1, bf16[512,1024]{1,0:T(8,128)(2,1)} %q_hbm.1, bf16[512,1024]{1,0:T(8,128)(2,1)} %k_hbm.1, bf16[512,1024]{1,0:T(8,128)(2,1)} %v_hbm.1, bf16[1024,4096]{1,0:T(8,128)(2,1)} %w_hbm.1, f32[8,128]{1,0:T(8,128)} %bitcast.3, ...), custom_call_target="tpu_custom_call" | custom-call | tf_op jit(solution)/shard_map/linear_attention_backward/pallas_call | solution.py:441
  168.5 0.0 copy-start
  168.5 2.8 %copy.11 = f32[128,3,1024]{2,0,1:T(8,128)} copy(f32[128,3,1024]{2,0,1:T(8,128)} %bitcast.2) | data formatting | bytes 3145728
  171.3 0.0 copy-done
  171.3 0.8 copy.12
Async XLA Ops:
  168.5 2.8 %copy-start = (f32[1024,128]{1,0:T(8,128)S(1)}, f32[1024,128]{1,0:T(8,128)}, u32[]{:S(2)}) copy-start(f32[1024,128]{1,0:T(8,128)} %get-tuple-element.9) | copy-start | bytes 1572868

commit v3 on v2

--- a/solution.py
+++ b/solution.py
@@ -70,16 +70,20 @@
         return pltpu.make_async_copy(
             w_hbm.at[:, pl.ds(start, width)], wbuf.at[n % 2], load_sem.at[5 + n])
 
-    order = (y, turn(y - 1), turn(y + 1), turn(y + 2))
+    order = (y, turn(y + 1), turn(y - 1), turn(y + 2))
+    late = order[3]
+
+    def arrival(source):
+        away = turn(source - y)
+        return away + lax.div(away, 2) * (5 - 2 * away)
+
     load_cot = pltpu.make_async_copy(cot_hbm, rown.at[1], load_sem.at[0])
     load_k = pltpu.make_async_copy(k_hbm, ks, load_sem.at[1])
     load_v = pltpu.make_async_copy(v_hbm, vs, load_sem.at[2])
     load_x = pltpu.make_async_copy(x_hbm, rown.at[2], load_sem.at[3])
     load_q = pltpu.make_async_copy(q_hbm, qs, load_sem.at[4])
-    for load in (load_cot, load_k, load_v, load_x, load_q):
+    for load in (load_cot, load_k, load_v):
         load.start()
-    weight_load(0, order[0]).start()
-    weight_load(1, order[1]).start()
 
     barrier = pltpu.get_barrier_semaphore()
     peers = [row_peer(turn(j + o, ROW)) for o in range(1, ROW)]
@@ -93,6 +97,10 @@
             lown[side, y, i // 2, i % 2] = rown[stage, :, i * HEAD_DIM:(i + 1) * HEAD_DIM].T
 
     load_cot.wait()
+    load_x.start()
+    load_q.start()
+    weight_load(0, order[0]).start()
+    weight_load(1, order[1]).start()
     transpose_in(0, 1)
     pl.semaphore_wait(barrier, len(peers))
 
@@ -182,6 +190,13 @@
     def put_head(comp, h, value):
         rown[comp, :, pl.ds(pl.multiple_of(h * HEAD_DIM, HEAD_DIM), HEAD_DIM)] = value.astype(BF16)
 
+    def left_swap(side, n):
+        return remote(lown.at[side, order[n], :, 1 - core], lpar.at[side, order[n]],
+                      lp_send.at[side, n], lp_recv.at[side, n], partner)
+
+    def right_swap(comp):
+        return remote(rown.at[comp], rpar.at[comp], rp_send.at[comp], rp_recv.at[comp], partner)
+
     load_k.wait()
     load_v.wait()
 
@@ -192,8 +207,9 @@
     scan_rows(0)
     load_x.wait()
     transpose_in(1, 2)
+    left_swap(0, 0).start()
+    left_swap(1, 0).start()
     load_q.wait()
-    scan_totals(0)
 
     lower_left = (
         lax.broadcasted_iota(jnp.int32, (tokens, half), 0)
@@ -202,19 +218,23 @@
     lower_right = lower_left[:half]
 
     def score_slots(h):
-        return lax.div(h, 2), lax.rem(h, 2) * 2
-
-    @pl.loop(0, heads)
-    def _(h):
-        q, k, v = head(qs, h), head(ks, h), head(vs, h)
-        left = jnp.where(lower_left, dot_nt(q, k[:half]), 0.0).astype(BF16)
-        right = jnp.where(lower_right, dot_nt(q[half:], k[half:]), 0.0).astype(BF16)
-        a, b = score_slots(h)
-        s1[a, b] = left
-        s1[a, b + 1, :half] = right
-        att[h, :half] = dot_nn(left[:half], v[:half])
-        att[h, half:] = dot_nn(left[half:], v[:half]) + dot_nn(right, v[half:])
-
+        return 1 + lax.div(h, 2), lax.rem(h, 2) * 2
+
+    def score_heads(begin, end):
+        @pl.loop(begin, end)
+        def _(h):
+            q, k, v = head(qs, h), head(ks, h), head(vs, h)
+            left = jnp.where(lower_left, dot_nt(q, k[:half]), 0.0).astype(BF16)
+            right = jnp.where(lower_right, dot_nt(q[half:], k[half:]), 0.0).astype(BF16)
+            a, b = score_slots(h)
+            s1[a, b] = left
+            s1[a, b + 1, :half] = right
+            att[h, :half] = dot_nn(left[:half], v[:half])
+            att[h, half:] = dot_nn(left[half:], v[:half]) + dot_nn(right, v[half:])
+
+    score_heads(0, heads // 2)
+    scan_totals(0)
+    score_heads(heads // 2, heads)
     scan_results(0)
 
     def grad_chunk(n):
@@ -233,9 +253,9 @@
         if n + 2 < RING:
             weight_load(n + 2, order[n + 2]).start()
 
-    grad_chunk(0)
     gather_pass(0)
     gather_own(1)
+    grad_chunk(0)
 
     def normalised(h):
         a = att[h]
@@ -250,25 +270,99 @@
         normed, _ = normalised(h)
         put_head(0, h, normed * gain_ref[pl.ds(h, 1), :])
 
-    def left_swap(side, piece):
-        return remote(lown.at[side, piece, :, 1 - core], lpar.at[side, piece],
-                      lp_send.at[side, piece], lp_recv.at[side, piece], partner)
-
-    def right_swap(comp):
-        return remote(rown.at[comp], rpar.at[comp], rp_send.at[comp], rp_recv.at[comp], partner)
-
     right_swap(0).start()
+
+    def term(comp, colour, d, groups=range(RING)):
+        side = lax.div(comp + 3, 4)
+        cut = slice(colour * cols, (colour + 1) * cols)
+        if COLOURS[colour][0]:
+            mine = jnp.concatenate([lown[side, order[n], d, core] for n in groups], axis=0)
+            other = jnp.concatenate([lpar[side, order[n], d] for n in groups], axis=0)
+        else:
+            mine = lown[side, d, :, core].reshape(rows, tokens)
+            other = lpar[side, d].reshape(rows, tokens)
+        return dot_nn(mine, rown[comp, :, cut]) + dot_nn(other, rpar[comp, :, cut])
+
+    def first_hop(k, comp, colour, part=0):
+        source = s1.at[comp, colour] if k == 0 else r1.at[k - 1, comp, colour]
+        target = r1.at[k, comp, colour]
+        if k == 0 and COLOURS[colour][0]:
+            piece = pl.ds(3 * HEAD_DIM, HEAD_DIM) if part else pl.ds(0, 3 * HEAD_DIM)
+            source, target = source.at[piece], target.at[piece]
+        return remote(source, target, s1_send.at[k + 3 * part, comp, colour],
+                      s1_recv.at[k + 3 * part, comp, colour], step_of(*COLOURS[colour]))
+
+    def second_place(colour, k):
+        is_z, sign = COLOURS[colour]
+        e = turn((x if is_z else z) - sign * (1 + k))
+        return arrival(e) if is_z else e
+
+    def second_hop(k, comp, colour):
+        is_z, sign = COLOURS[colour]
+        source = acc.at[comp, colour, second_place(colour, 0)] if k == 0 else r2.at[k - 1, comp, colour]
+        return remote(source, r2.at[k, comp, colour], s2_send.at[k, comp, colour],
+                      s2_recv.at[k, comp, colour], step_of(not is_z, sign))
+
+    def zero_step(comp, part):
+        for colour in (0, 1):
+            d = turn(z - COLOURS[colour][1])
+            groups = range(3, 4) if part else range(3)
+            piece = slice(3 * HEAD_DIM, rows) if part else slice(0, 3 * HEAD_DIM)
+            s1[comp, colour, piece] = term(comp, colour, d, groups).astype(BF16)
+        for colour in (0, 1):
+            first_hop(0, comp, colour, part).start()
+        for colour in (2, 3):
+            d = turn(x - COLOURS[colour][1])
+
+            @pl.when((d == late) if part else (d != late))
+            def _(colour=colour, d=d):
+                s1[comp, colour] = term(comp, colour, d).astype(BF16)
+                first_hop(0, comp, colour).start()
+
+    def first_step(k, comp):
+        for colour, (is_z, sign) in enumerate(COLOURS):
+            value = term(comp, colour, turn((z if is_z else x) - sign * (1 + k)))
+            first_hop(k - 1, comp, colour).wait_recv()
+            if k == 1 and is_z:
+                first_hop(0, comp, colour, 1).wait_recv()
+            value = (value + r1[k - 1, comp, colour].astype(F32)).astype(BF16)
+            if k < RING - 1:
+                r1[k - 1, comp, colour] = value
+            else:
+                acc[comp, colour] = value.reshape(RING, HEAD_DIM, cols)
+        for colour in range(4):
+            if k < RING - 1:
+                first_hop(k, comp, colour).start()
+            else:
+                second_hop(0, comp, colour).start()
+
+    def second_value(k, comp, colour):
+        second_hop(k - 1, comp, colour).wait_recv()
+        return (acc[comp, colour, second_place(colour, k)].astype(F32)
+                + r2[k - 1, comp, colour].astype(F32))
+
+    def second_step(k, comp):
+        for colour in range(4):
+            r2[k - 1, comp, colour] = second_value(k, comp, colour).astype(BF16)
+        for colour in range(4):
+            second_hop(k, comp, colour).start()
+
+    ring(0, -1, 1, True).wait_recv()
+    left_swap(0, 1).start()
+    grad_chunk(1)
     ring(0, 1, 1, True).wait_recv()
-    left_swap(0, order[0]).start()
-    left_swap(0, order[1]).start()
-    grad_chunk(1)
-    ring(0, -1, 1, True).wait_recv()
-    left_swap(0, order[2]).start()
+    left_swap(0, 2).start()
     grad_chunk(2)
+    for n in range(3):
+        left_swap(0, n).wait_recv()
+    right_swap(0).wait_recv()
+    zero_step(0, 0)
     ring(0, 1, 2, True).wait_recv()
     ring(0, -1, 2, True).wait_recv()
-    left_swap(0, order[3]).start()
+    left_swap(0, 3).start()
     grad_chunk(3)
+    left_swap(0, 3).wait_recv()
+    zero_step(0, 1)
 
     @pl.loop(0, heads)
     def _(h):
@@ -281,85 +375,31 @@
 
     scan_rows(1)
 
-    def term(comp, colour, d):
-        side = lax.div(comp + 3, 4)
-        cut = slice(colour * cols, (colour + 1) * cols)
-        if COLOURS[colour][0]:
-            mine, other = lown[side, :, d, core], lpar[side, :, d]
-        else:
-            mine, other = lown[side, d, :, core], lpar[side, d]
-        value = dot_nn(mine.reshape(rows, tokens), rown[comp, :, cut])
-        return value + dot_nn(other.reshape(rows, tokens), rpar[comp, :, cut])
-
-    def first_hop(k, comp, colour):
-        source = s1.at[comp, colour] if k == 0 else r1.at[k - 1, comp, colour]
-        return remote(source, r1.at[k, comp, colour], s1_send.at[k, comp, colour],
-                      s1_recv.at[k, comp, colour], step_of(*COLOURS[colour]))
-
-    def second_hop(k, comp, colour):
-        is_z, sign = COLOURS[colour]
-        place = x if is_z else z
-        source = acc.at[comp, colour, turn(place - sign)] if k == 0 else r2.at[k - 1, comp, colour]
-        return remote(source, r2.at[k, comp, colour], s2_send.at[k, comp, colour],
-                      s2_recv.at[k, comp, colour], step_of(not is_z, sign))
-
-    def first_step(k, comp):
-        for colour, (is_z, sign) in enumerate(COLOURS):
-            value = term(comp, colour, turn((z if is_z else x) - sign * (1 + k)))
-            if k:
-                first_hop(k - 1, comp, colour).wait_recv()
-                value = value + r1[k - 1, comp, colour].astype(F32)
-            value = value.astype(BF16)
-            if k == 0:
-                s1[comp, colour] = value
-            elif k < RING - 1:
-                r1[k - 1, comp, colour] = value
-            else:
-                acc[comp, colour] = value.reshape(RING, HEAD_DIM, cols)
-        for colour in range(4):
-            if k < RING - 1:
-                first_hop(k, comp, colour).start()
-            else:
-                second_hop(0, comp, colour).start()
-
-    def second_value(k, comp, colour):
-        is_z, sign = COLOURS[colour]
-        e = turn((x if is_z else z) - sign * (1 + k))
-        second_hop(k - 1, comp, colour).wait_recv()
-        return acc[comp, colour, e].astype(F32) + r2[k - 1, comp, colour].astype(F32)
-
-    def second_step(k, comp):
-        for colour in range(4):
-            r2[k - 1, comp, colour] = second_value(k, comp, colour).astype(BF16)
-        for colour in range(4):
-            second_hop(k, comp, colour).start()
-
+    def mixing_heads(begin, end):
+        @pl.loop(begin, end)
+        def _(h):
+            q, k, v, p = head(qs, h), head(ks, h), head(vs, h), pre[h]
+            state = states[0, h]
+            left = jnp.where(lower_left, dot_nt(p, v[:half]), 0.0).astype(BF16)
+            right = jnp.where(lower_right, dot_nt(p[half:], v[half:]), 0.0).astype(BF16)
+            low = dot_nn(left, k[:half]) + dot_nt(p, state)
+            cut = pl.ds(pl.multiple_of(h * HEAD_DIM, HEAD_DIM), HEAD_DIM)
+            rown[1, :half, cut] = low[:half].astype(BF16)
+            rown[1, half:, cut] = (low[half:] + dot_nn(right, k[half:])).astype(BF16)
+            att[h, :half] = dot_tn(left, q)
+            att[h, half:] = dot_tn(right, q[half:])
+            a, b = score_slots(h)
+            gg[h, :half] = dot_tn(s1[a, b], p)
+            gg[h, half:] = dot_tn(s1[a, b + 1, :half], p[half:])
+
+    mixing_heads(0, heads // 2)
     scan_totals(1)
-
-    @pl.loop(0, heads)
-    def _(h):
-        q, k, v, p = head(qs, h), head(ks, h), head(vs, h), pre[h]
-        state = states[0, h]
-        left = jnp.where(lower_left, dot_nt(p, v[:half]), 0.0).astype(BF16)
-        right = jnp.where(lower_right, dot_nt(p[half:], v[half:]), 0.0).astype(BF16)
-        old = dot_nt(p, state)
-        low = dot_nn(left, k[:half]) + old
-        cut = pl.ds(pl.multiple_of(h * HEAD_DIM, HEAD_DIM), HEAD_DIM)
-        rown[1, :half, cut] = low[:half].astype(BF16)
-        rown[1, half:, cut] = (low[half:] + dot_nn(right, k[half:])).astype(BF16)
-        att[h, :half] = dot_tn(left, q)
-        att[h, half:] = dot_tn(right, q[half:])
-        a, b = score_slots(h)
-        gg[h, :half] = dot_tn(s1[a, b], p)
-        gg[h, half:] = dot_tn(s1[a, b + 1, :half], p[half:])
-
+    first_step(1, 0)
+    mixing_heads(heads // 2, heads)
+    right_swap(1).start()
     scan_results(1)
-    right_swap(1).start()
-    for piece in order:
-        left_swap(0, piece).wait_recv()
-    right_swap(0).wait_recv()
-    first_step(0, 0)
     gather_pass(1)
+    first_step(2, 0)
     scan_end(1)
 
     @pl.loop(0, heads)
@@ -370,33 +410,38 @@
 
     right_swap(2).start()
     right_swap(3).start()
-    first_step(1, 0)
-    left_swap(1, order[0]).start()
+    ring(1, -1, 1, True).wait_recv()
+    left_swap(1, 1).start()
     ring(1, 1, 1, True).wait_recv()
-    left_swap(1, order[1]).start()
-    ring(1, -1, 1, True).wait_recv()
-    left_swap(1, order[2]).start()
-    first_step(2, 0)
+    left_swap(1, 2).start()
+    first_step(3, 0)
+    for n in range(3):
+        left_swap(1, n).wait_recv()
+
+    @pl.loop(1, 4)
+    def _(comp):
+        right_swap(comp).wait_recv()
+        zero_step(comp, 0)
+
+    second_step(1, 0)
     ring(1, 1, 2, True).wait_recv()
     ring(1, -1, 2, True).wait_recv()
-    left_swap(1, order[3]).start()
-    first_step(3, 0)
-    for comp in range(1, 4):
-        right_swap(comp).wait_recv()
-    for piece in order:
-        left_swap(1, piece).wait_recv()
-
-    for k in range(RING):
+    left_swap(1, 3).start()
+    second_step(2, 0)
+    left_swap(1, 3).wait_recv()
+
+    @pl.loop(1, 4)
+    def _(comp):
+        zero_step(comp, 1)
+
+    for colour in range(4):
+        cut = slice(colour * cols, (colour + 1) * cols)
+        out_ref[cut, :] = second_value(RING - 1, 0, colour).T
+
+    for k in range(1, RING):
         @pl.loop(1, 4)
         def _(comp, k=k):
             first_step(k, comp)
-
-        if 0 < k < RING - 1:
-            second_step(k, 0)
-
-    for colour in range(4):
-        cut = slice(colour * cols, (colour + 1) * cols)
-        out_ref[cut, :] = second_value(RING - 1, 0, colour).T
 
     for k in range(1, RING - 1):
         @pl.loop(1, 4)
@@ -413,8 +458,8 @@
         for sign in (1, -1):
             for message in range(3):
                 ring(side, sign, message).wait_send()
-        for piece in order:
-            left_swap(side, piece).wait_send()
+        for n in range(RING):
+            left_swap(side, n).wait_send()
         for o in range(1, ROW):
             row_copy(side, o).wait_send()
             result_copy(side, o).wait_send()
@@ -428,6 +473,8 @@
             for k in range(RING - 1):
                 first_hop(k, comp, colour).wait_send()
                 second_hop(k, comp, colour).wait_send()
+            if COLOURS[colour][0]:
+                first_hop(0, comp, colour, 1).wait_send()
 
 
 def body(layer_input, query_rows, key_rows, value_rows, out_weight, norm_gain, cotangent):
@@ -458,7 +505,7 @@
             pltpu.VMEM((heads, tokens, HEAD_DIM), F32),
             pltpu.VMEM((heads, tokens, HEAD_DIM), F32),
             pltpu.VMEM((heads, tokens, HEAD_DIM), BF16),
-            pltpu.VMEM((4, 4, RING * HEAD_DIM, cols), BF16),
+            pltpu.VMEM((5, 4, RING * HEAD_DIM, cols), BF16),
             pltpu.VMEM((RING - 1, 4, 4, RING * HEAD_DIM, cols), BF16),
             pltpu.VMEM((4, 4, RING, HEAD_DIM, cols), BF16),
             pltpu.VMEM((RING - 1, 4, 4, HEAD_DIM, cols), BF16),
@@ -474,7 +521,7 @@
             dma((2, ROW - 1)), dma((2, ROW - 1)),
             dma((2, RING)), dma((2, RING)),
             dma((4,)), dma((4,)),
-            dma((RING - 1, 4, 4)), dma((RING - 1, 4, 4)),
+            dma((RING, 4, 4)), dma((RING, 4, 4)),
             dma((RING - 1, 4, 4)), dma((RING - 1, 4, 4)),
         ],
         compiler_params=pltpu.CompilerParams(

time: 172 us -> 180 us (1.047)
  Pallas kernels: 168 us -> 176 us
    pallas_call x1, Pallas kernels: 168 us -> 176 us  [body(): pl.pallas_call(step_kernel, out_shape=(jax.ShapeDtypeStruct((3, HEAD_DIM,...]
where the time goes in v3:
time: 180 us
  Pallas kernels  176 us (98%)
  local copies, waits for them, and re-layouts  3.58 us (2%)
    pallas_call x1, Pallas kernels, body(): pl.pallas_call(step_kernel, out_shape=(jax.ShapeDtypeStruct((3, HEAD_DIM,...  176 us

profile of v3, /device:TPU:0, one launch (start us, length us, event | category | flops | bytes accessed | tf_op | source)
XLA Modules:
  0.0 180.2 jit_solution(9759360649546901639)
XLA Ops:
  0.6 176.0 %linear_attention_backward.1 = (f32[3,128,1024]{2,1,0:T(8,128)}, f32[1024,128]{1,0:T(8,128)}) custom-call(bf16[512,1024]{1,0:T(8,128)(2,1)} %x_hbm.1, bf16[512,1024]{1,0:T(8,128)(2,1)} %q_hbm.1, bf16[512,1024]{1,0:T(8,128)(2,1)} %k_hbm.1, bf16[512,1024]{1,0:T(8,128)(2,1)} %v_hbm.1, bf16[1024,4096]{1,0:T(8,128)(2,1)} %w_hbm.1, f32[8,128]{1,0:T(8,128)} %bitcast.3, ...), custom_call_target="tpu_custom_call" | custom-call | tf_op jit(solution)/shard_map/linear_attention_backward/pallas_call | solution.py:488
  176.6 0.0 copy-start
  176.6 2.8 %copy.11 = f32[128,3,1024]{2,0,1:T(8,128)} copy(f32[128,3,1024]{2,0,1:T(8,128)} %bitcast.2) | data formatting | bytes 3145728
  179.4 0.0 copy-done
  179.4 0.8 copy.12
Async XLA Ops:
  176.6 2.8 %copy-start = (f32[1024,128]{1,0:T(8,128)S(1)}, f32[1024,128]{1,0:T(8,128)}, u32[]{:S(2)}) copy-start(f32[1024,128]{1,0:T(8,128)} %get-tuple-element.9) | copy-start | bytes 1572868

commit v4 on v3

--- a/solution.py
+++ b/solution.py
@@ -353,16 +353,10 @@
     ring(0, 1, 1, True).wait_recv()
     left_swap(0, 2).start()
     grad_chunk(2)
-    for n in range(3):
-        left_swap(0, n).wait_recv()
-    right_swap(0).wait_recv()
-    zero_step(0, 0)
     ring(0, 1, 2, True).wait_recv()
     ring(0, -1, 2, True).wait_recv()
     left_swap(0, 3).start()
     grad_chunk(3)
-    left_swap(0, 3).wait_recv()
-    zero_step(0, 1)
 
     @pl.loop(0, heads)
     def _(h):
@@ -394,12 +388,15 @@
 
     mixing_heads(0, heads // 2)
     scan_totals(1)
-    first_step(1, 0)
     mixing_heads(heads // 2, heads)
     right_swap(1).start()
+    gather_pass(1)
     scan_results(1)
-    gather_pass(1)
-    first_step(2, 0)
+    for n in range(RING):
+        left_swap(0, n).wait_recv()
+    right_swap(0).wait_recv()
+    zero_step(0, 0)
+    zero_step(0, 1)
     scan_end(1)
 
     @pl.loop(0, heads)
@@ -410,11 +407,11 @@
 
     right_swap(2).start()
     right_swap(3).start()
+    first_step(1, 0)
     ring(1, -1, 1, True).wait_recv()
     left_swap(1, 1).start()
     ring(1, 1, 1, True).wait_recv()
     left_swap(1, 2).start()
-    first_step(3, 0)
     for n in range(3):
         left_swap(1, n).wait_recv()
 
@@ -423,25 +420,28 @@
         right_swap(comp).wait_recv()
         zero_step(comp, 0)
 
-    second_step(1, 0)
+    first_step(2, 0)
     ring(1, 1, 2, True).wait_recv()
     ring(1, -1, 2, True).wait_recv()
     left_swap(1, 3).start()
-    second_step(2, 0)
+    first_step(3, 0)
     left_swap(1, 3).wait_recv()
 
     @pl.loop(1, 4)
     def _(comp):
         zero_step(comp, 1)
-
-    for colour in range(4):
-        cut = slice(colour * cols, (colour + 1) * cols)
-        out_ref[cut, :] = second_value(RING - 1, 0, colour).T
 
     for k in range(1, RING):
         @pl.loop(1, 4)
         def _(comp, k=k):
             first_step(k, comp)
+
+        if k < RING - 1:
+            second_step(k, 0)
+
+    for colour in range(4):
+        cut = slice(colour * cols, (colour + 1) * cols)
+        out_ref[cut, :] = second_value(RING - 1, 0, colour).T
 
     for k in range(1, RING - 1):
         @pl.loop(1, 4)

time: 180 us -> 184 us (1.022)
  Pallas kernels: 176 us -> 179 us
    pallas_call x1, Pallas kernels: 176 us -> 179 us  [body(): pl.pallas_call(step_kernel, out_shape=(jax.ShapeDtypeStruct((3, HEAD_DIM,...]
where the time goes in v4:
time: 184 us; the launch traced here: 183 us
  Pallas kernels  179 us (97%)
  local copies, waits for them, and re-layouts  3.58 us (2%)
    pallas_call x1, Pallas kernels, body(): pl.pallas_call(step_kernel, out_shape=(jax.ShapeDtypeStruct((3, HEAD_DIM,...  179 us

profile of v4, /device:TPU:0, one launch (start us, length us, event | category | flops | bytes accessed | tf_op | source)
XLA Modules:
  0.0 183.5 jit_solution(14878739424774164827)
XLA Ops:
  0.6 179.2 %linear_attention_backward.1 = (f32[3,128,1024]{2,1,0:T(8,128)}, f32[1024,128]{1,0:T(8,128)}) custom-call(bf16[512,1024]{1,0:T(8,128)(2,1)} %x_hbm.1, bf16[512,1024]{1,0:T(8,128)(2,1)} %q_hbm.1, bf16[512,1024]{1,0:T(8,128)(2,1)} %k_hbm.1, bf16[512,1024]{1,0:T(8,128)(2,1)} %v_hbm.1, bf16[1024,4096]{1,0:T(8,128)(2,1)} %w_hbm.1, f32[8,128]{1,0:T(8,128)} %bitcast.3, ...), custom_call_target="tpu_custom_call" | custom-call | tf_op jit(solution)/shard_map/linear_attention_backward/pallas_call | solution.py:488
  179.9 0.0 copy-start
  179.9 2.8 %copy.11 = f32[128,3,1024]{2,0,1:T(8,128)} copy(f32[128,3,1024]{2,0,1:T(8,128)} %bitcast.2) | data formatting | bytes 3145728
  182.7 0.0 copy-done
  182.7 0.8 copy.12
Async XLA Ops:
  179.9 2.8 %copy-start = (f32[1024,128]{1,0:T(8,128)S(1)}, f32[1024,128]{1,0:T(8,128)}, u32[]{:S(2)}) copy-start(f32[1024,128]{1,0:T(8,128)} %get-tuple-element.9) | copy-start | bytes 1572868

commit v5 on v2

--- a/solution.py
+++ b/solution.py
@@ -76,10 +76,8 @@
     load_v = pltpu.make_async_copy(v_hbm, vs, load_sem.at[2])
     load_x = pltpu.make_async_copy(x_hbm, rown.at[2], load_sem.at[3])
     load_q = pltpu.make_async_copy(q_hbm, qs, load_sem.at[4])
-    for load in (load_cot, load_k, load_v, load_x, load_q):
+    for load in (load_cot, load_k, load_v):
         load.start()
-    weight_load(0, order[0]).start()
-    weight_load(1, order[1]).start()
 
     barrier = pltpu.get_barrier_semaphore()
     peers = [row_peer(turn(j + o, ROW)) for o in range(1, ROW)]
@@ -93,6 +91,10 @@
             lown[side, y, i // 2, i % 2] = rown[stage, :, i * HEAD_DIM:(i + 1) * HEAD_DIM].T
 
     load_cot.wait()
+    load_x.start()
+    load_q.start()
+    weight_load(0, order[0]).start()
+    weight_load(1, order[1]).start()
     transpose_in(0, 1)
     pl.semaphore_wait(barrier, len(peers))
 
@@ -233,9 +235,9 @@
         if n + 2 < RING:
             weight_load(n + 2, order[n + 2]).start()
 
-    grad_chunk(0)
     gather_pass(0)
     gather_own(1)
+    grad_chunk(0)
 
     def normalised(h):
         a = att[h]
@@ -355,11 +357,11 @@
 
     scan_results(1)
     right_swap(1).start()
+    gather_pass(1)
     for piece in order:
         left_swap(0, piece).wait_recv()
     right_swap(0).wait_recv()
     first_step(0, 0)
-    gather_pass(1)
     scan_end(1)
 
     @pl.loop(0, heads)

time: 172 us -> 172 us (level)
  no operation moved by 1% of the time
where the time goes in v5:
time: 172 us
  Pallas kernels  168 us (98%)
  local copies, waits for them, and re-layouts  3.58 us (2%)
    pallas_call x1, Pallas kernels, body(): pl.pallas_call(step_kernel, out_shape=(jax.ShapeDtypeStruct((3, HEAD_DIM,...  168 us
    unnamed x4, local copies, waits for them, and re-layouts  3.58 us

profile of v5, /device:TPU:0, one launch (start us, length us, event | category | flops | bytes accessed | tf_op | source)
XLA Modules:
  0.0 172.0 jit_solution(1024107378779469559)
XLA Ops:
  0.6 167.8 %linear_attention_backward.1 = (f32[3,128,1024]{2,1,0:T(8,128)}, f32[1024,128]{1,0:T(8,128)}) custom-call(bf16[512,1024]{1,0:T(8,128)(2,1)} %x_hbm.1, bf16[512,1024]{1,0:T(8,128)(2,1)} %q_hbm.1, bf16[512,1024]{1,0:T(8,128)(2,1)} %k_hbm.1, bf16[512,1024]{1,0:T(8,128)(2,1)} %v_hbm.1, bf16[1024,4096]{1,0:T(8,128)(2,1)} %w_hbm.1, f32[8,128]{1,0:T(8,128)} %bitcast.3, ...), custom_call_target="tpu_custom_call" | custom-call | tf_op jit(solution)/shard_map/linear_attention_backward/pallas_call | solution.py:443
  168.4 0.0 copy-start
  168.4 2.8 %copy.11 = f32[128,3,1024]{2,0,1:T(8,128)} copy(f32[128,3,1024]{2,0,1:T(8,128)} %bitcast.2) | data formatting | bytes 3145728
  171.2 0.0 copy-done
  171.2 0.8 copy.12
Async XLA Ops:
  168.4 2.8 %copy-start = (f32[1024,128]{1,0:T(8,128)S(1)}, f32[1024,128]{1,0:T(8,128)}, u32[]{:S(2)}) copy-start(f32[1024,128]{1,0:T(8,128)} %get-tuple-element.9) | copy-start | bytes 1572868
